TPU v7x, 32 devices: a whole 2x2x4 slice. The times are simulated.
32 devices in a mesh: band: 4 (over z), head: 4 (over y, x), dp: 2 (over core).
Axes of the slice: x: 2, y: 2, z: 4, core: 2. Of those that a mesh axis runs over, the one named last changes fastest.
Arguments:
- tokens: bfloat16 [32, 1024, 512], P(('dp', 'band'), None, 'head'), parts along dimension 0, may hold values from -6 to 6
- corner_row: int32 [2048], P('dp'), parts along dimension 0, may hold values from 0 to 14
- corner_col: int32 [2048], P('dp'), parts along dimension 0, may hold values from 0 to 1022
- fraction: float32 [2, 2048], P(None, 'dp'), parts along dimension 1, may hold values from 0 to 1
- w_query: bfloat16 [512, 512], P(None, 'head'), may hold values from -2 to 2
- w_key: bfloat16 [512, 512], P(None, 'head'), may hold values from -2 to 2
- w_value: bfloat16 [512, 512], P(None, 'head'), may hold values from -0.25 to 0.25
- w_out: bfloat16 [512, 512], P('head'), may hold values from -0.25 to 0.25
- conv_kernel: float32 [25, 512], P(None, 'head'), may hold values from -1.25 to 1.25
- norm_gain: float32 [512], replicated, may hold values from 0.1 to 1.9
Outputs:
- mixed: bfloat16 [32, 1024, 512], P(('dp', 'band'), None, 'head'), parts along dimension 0
There are 2 independent parts, one for each index of `dp`. A program takes and returns all parts, laid end to end along the dimension named above; an argument that names none is the same for every part. Nothing has to cross between parts.
All inputs are finite; a program needn't handle non-finite values.
Results may differ from a plain program's by a relative error of at most 0.029.
Values may be sent and summed in bfloat16 or wider, within the bound.
A program may use at most 64 MiB of HBM per device.

v0:
```python
import jax
import jax.numpy as jnp
from jax import lax
from jax.sharding import PartitionSpec as P

HEADS = 16
KER = 5


def padded_2(block, sides, width):
    for axis, dim in sides:
        count = lax.axis_size(axis)
        forward = [(i, i + 1) for i in range(count - 1)]
        backward = [(target, source) for source, target in forward]
        low = lax.ppermute(
            lax.slice_in_dim(block, block.shape[dim] - width, None, axis=dim), axis, forward
        )
        high = lax.ppermute(lax.slice_in_dim(block, 0, width, axis=dim), axis, backward)
        block = jnp.concatenate([low, block, high], axis=dim)
    return block


def layer_norm(values, norm_gain):
    values = values.astype(jnp.float32)
    center = jnp.mean(values, axis=-1, keepdims=True)
    spread = jnp.mean(jnp.square(values - center), axis=-1, keepdims=True)
    return ((values - center) * lax.rsqrt(spread + 1e-05) * norm_gain).astype(jnp.bfloat16)


def sample_points(normed, col_table, row_table, count):

    def add_row(index, total):
        plane = lax.dynamic_index_in_dim(normed, index, 0, keepdims=False)
        inner = jnp.dot(col_table, plane, preferred_element_type=jnp.float32)
        weight = lax.dynamic_index_in_dim(row_table, index, 1, keepdims=True)
        return total + weight * inner

    empty = jnp.zeros((count, normed.shape[2]), jnp.float32)
    return lax.fori_loop(0, normed.shape[0], add_row, empty)


def attend(query, key, value, heads):
    count, width = query.shape
    size = width // heads
    block = min(512, count)
    blocks = query.reshape(count // block, block, heads, size)
    key_heads = key.reshape(-1, heads, size)
    value_heads = value.reshape(-1, heads, size)
    scale = 1.0 / size**0.5

    def one_block(part):
        scores = (
            jnp.einsum("qhd,khd->hqk", part, key_heads, preferred_element_type=jnp.float32) * scale
        )
        top = jnp.max(scores, axis=-1, keepdims=True)
        expo = jnp.exp(scores - top)
        probs = (expo / jnp.sum(expo, axis=-1, keepdims=True)).astype(jnp.bfloat16)
        out = jnp.einsum("hqk,khd->qhd", probs, value_heads, preferred_element_type=jnp.float32)
        return out.astype(jnp.bfloat16).reshape(block, width)

    return lax.map(one_block, blocks).reshape(count, width)


def shards(
    tokens, corner_row, corner_col, fraction, w_query, w_key, w_value, w_out, conv_kernel, norm_gain
):
    band_rows, columns, channels = tokens.shape
    whole = lax.all_gather(tokens, "head", axis=2, tiled=True)
    normed = layer_norm(whole, norm_gain)
    width = normed.shape[2]
    count = band_rows * columns
    query = jnp.dot(
        normed.reshape(count, width), w_query, preferred_element_type=jnp.float32
    ).astype(jnp.bfloat16)
    channel_start = lax.axis_index("head") * channels
    normed_here = lax.dynamic_slice_in_dim(normed, channel_start, channels, 2)
    row_top = (1.0 - fraction[0]).astype(jnp.bfloat16)
    row_bottom = fraction[0].astype(jnp.bfloat16)
    col_left = (1.0 - fraction[1]).astype(jnp.bfloat16)
    col_right = fraction[1].astype(jnp.bfloat16)
    positions = lax.broadcasted_iota(jnp.int32, (1, columns), 1)
    zero_bf = jnp.zeros((), jnp.bfloat16)
    col_table = jnp.where(positions == corner_col[:, None], col_left[:, None], zero_bf) + jnp.where(
        positions == corner_col[:, None] + 1, col_right[:, None], zero_bf
    )
    band_start = lax.axis_index("band") * band_rows
    grid_rows = band_start + lax.broadcasted_iota(jnp.int32, (1, band_rows), 1)
    zero_f = jnp.zeros((), jnp.float32)
    row_table = jnp.where(
        grid_rows == corner_row[:, None], row_top.astype(jnp.float32)[:, None], zero_f
    ) + jnp.where(
        grid_rows == corner_row[:, None] + 1, row_bottom.astype(jnp.float32)[:, None], zero_f
    )
    points = corner_row.shape[0]
    share_rows = points // lax.axis_size("band")
    piece = lax.psum_scatter(
        sample_points(normed_here, col_table, row_table, share_rows * lax.axis_size("band")).astype(
            jnp.bfloat16
        ),
        "band",
        scatter_dimension=0,
        tiled=True,
    )
    share = lax.all_gather(piece, "head", axis=1, tiled=True)
    key_share = jnp.dot(share, w_key, preferred_element_type=jnp.float32).astype(jnp.bfloat16)
    value_share = jnp.dot(share, w_value, preferred_element_type=jnp.float32).astype(jnp.bfloat16)
    key, value = (
        lax.all_gather(key_share, "band", axis=0, tiled=True),
        lax.all_gather(value_share, "band", axis=0, tiled=True),
    )
    heads_here = HEADS // lax.axis_size("head")
    attended = attend(query, key, value, heads_here)
    partial_out = jnp.dot(attended, w_out, preferred_element_type=jnp.float32).reshape(
        band_rows, columns, width
    )
    projected = lax.psum_scatter(
        partial_out.astype(jnp.bfloat16), "head", scatter_dimension=2, tiled=True
    ).astype(jnp.float32)
    margin = KER // 2
    rimmed = padded_2(normed_here, (("band", 0),), margin)
    padded = jnp.pad(rimmed, ((0, 0), (margin, margin), (0, 0))).astype(jnp.float32)
    local = jnp.zeros((band_rows, columns, channels), jnp.float32)
    for first in range(KER):
        for second in range(KER):
            local = (
                local
                + conv_kernel[first * KER + second]
                * padded[first : first + band_rows, second : second + columns]
            )
    total = tokens.astype(jnp.float32) + projected + local
    return total.astype(jnp.bfloat16)


def solution(mesh):
    return jax.shard_map(
        shards,
        mesh=mesh,
        in_specs=(
            P(("dp", "band"), None, "head"),
            P("dp"),
            P("dp"),
            P(None, "dp"),
            P(None, "head"),
            P(None, "head"),
            P(None, "head"),
            P("head", None),
            P(None, "head"),
            P(),
        ),
        out_specs=P(("dp", "band"), None, "head"),
        check_vma=False,
    )
```

profile of v0, /device:TPU:0, one launch (start us, length us, event | category | flops | bytes accessed | tf_op | source)
XLA Modules:
  0.0 302.1 jit_solution(5138590391112813641)
XLA Ops:
  11.0 53.4 %all-gather.2.cloned.1.call-done = bf16[4,1024,512]{2,1,0:T(8,128)(2,1)} async-done(((bf16[4,1024,128]{2,1,0:T(8,128)(2,1)}), bf16[4,1024,512]{2,1,0:T(8,128)(2,1)}) %all-gather.2.cloned.1.call-update) | async-done | bytes 4194320 | tf_op jit(solution)/shard_map/all_gather | solution.py:68
  64.4 3.0 convert_reduce_fusion
  73.7 6.7 %while.25 = (s32[]{:T(128)}, f32[1024,128]{0,1:T(8,128)S(1)}, f32[1024,4]{0,1:T(4,128)S(1)}, bf16[4,1024,128]{2,1,0:T(8,128)(2,1)S(1)}, s32[1024]{0:T(1024)S(1)}...) while((s32[]{:T(128)}, f32[1024,128]{0,1:T(8,128)S(1)}, ...), condition=%wide.region_3.4_spmd.clone, body=%wide.region_2.3_spmd.clone.sunk | while | flops 277217280 | bytes 1335423 | solution.py:39
  81.2 3.4 %convolution_convert_fusion = bf16[4096,128]{1,0:T(8,128)(2,1)S(1)} fusion(bf16[4096,512]{1,0:T(8,128)(2,1)} %bitcast.130, bf16[512,128]{1,0:T(8,128)(2,1)S(1)} %copy-done.4), kind=kOutput, calls=%fused_computation.50 | convolution fusion | flops 537395200 | bytes 5373952 | tf_op jit(solution)/shard_map/dot_general | solution.py:72
  85.9 15.3 %reduce-scatter.5.cloned.1.call-done = bf16[256,128]{0,1:T(8,128)(2,1)} async-done(((bf16[1024,128]{0,1:T(8,128)(2,1)}), bf16[256,128]{0,1:T(8,128)(2,1)}) %reduce-scatter.5.cloned.1.call-update) | async-done | bytes 65552 | tf_op jit(solution)/shard_map/reduce_scatter | solution.py:96
  101.3 9.2 %all_gather.13 = bf16[256,512]{0,1:T(8,128)(2,1)S(1)} all-gather(bf16[256,128]{0,1:T(8,128)(2,1)} %reduce-scatter.5.cloned.1.call-done), channel_id=1, replica_groups=mesh['band'=4,'head'=4,'dp'=2] {'head'}, dimensions={1}, use_global_device_ids=true | all-gather | bytes 327680 | tf_op jit(solution)/shard_map/all_gather | solution.py:104
  111.0 14.3 %all_gather.14 = bf16[1024,128]{1,0:T(8,128)(2,1)S(1)} all-gather(bf16[256,128]{1,0:T(8,128)(2,1)S(1)} %convolution_convert_fusion.3), channel_id=1, replica_groups=mesh['band'=4,'head'=4,'dp'=2] {'band'}, dimensions={0}, use_global_device_ids=true | all-gather | bytes 327680 | tf_op jit(solution)/shard_map/all_gather | solution.py:108
  125.5 14.0 %all_gather.15 = bf16[1024,128]{1,0:T(8,128)(2,1)S(1)} all-gather(bf16[256,128]{1,0:T(8,128)(2,1)S(1)} %convolution_convert_fusion.2), channel_id=1, replica_groups=mesh['band'=4,'head'=4,'dp'=2] {'band'}, dimensions={0}, use_global_device_ids=true | all-gather | bytes 327680 | tf_op jit(solution)/shard_map/all_gather | solution.py:109
  139.7 54.7 %while.24 = (s32[]{:T(128)}, bf16[8,512,128]{2,1,0:T(8,128)(2,1)}, bf16[8,512,4,32]{1,3,2,0:T(8,128)(2,1)S(1)}, bf16[1024,4,32]{0,2,1:T(8,128)(2,1)S(1)}, bf16[1024,4,32]{0,2,1:T(8,128)(2,1)S(1)}, /*index=5*/s32[]{:T(128)}) while((s32[]{:T(128)}, bf16[8,512,128]{2,1,0:T(8,128)(2,1)}, bf16[8,512,4,32]{1,3,2,0:T(8,128)(2,1)S(1)}, ...), condition=%wide.region_8.9_spmd, body=%wide.region_5.8_spmd.sunk | while | flops 417402880 | bytes 1720409 | solution.py:61
  139.7 2.9 fusion.147
  142.6 3.1 %fusion.148 = bf16[4,512,32]{1,2,0:T(8,128)(2,1)S(1)} fusion(bf16[1024,4,32]{0,2,1:T(8,128)(2,1)S(1)} %get-tuple-element.358, f32[4,512]{1,0:T(4,128)S(1)} %fusion.147, bf16[1024,4,32]{0,2,1:T(8,128)(2,1)S(1)} %get-tuple-element.357, bf16[8,512,4,32]{1,3,2,0:T(8,128)(2,1)S(1)} %get-tuple-element.356, s32[]{:T(128)S(6)} %copy.42), kind=kOutput, calls=%fused_computation.8.clone.1 | convolution fusion | flops 276892672 | bytes 794628 | tf_op jit(solution)/shard_map/while/body/eval_jaxpr/hqk,khd->qhd/dot_general | solution.py:58
  146.5 2.9 fusion.147
  149.5 3.1 %fusion.148 = bf16[4,512,32]{1,2,0:T(8,128)(2,1)S(1)} fusion(bf16[1024,4,32]{0,2,1:T(8,128)(2,1)S(1)} %get-tuple-element.358, f32[4,512]{1,0:T(4,128)S(1)} %fusion.147, bf16[1024,4,32]{0,2,1:T(8,128)(2,1)S(1)} %get-tuple-element.357, bf16[8,512,4,32]{1,3,2,0:T(8,128)(2,1)S(1)} %get-tuple-element.356, s32[]{:T(128)S(6)} %copy.42), kind=kOutput, calls=%fused_computation.8.clone.1 | convolution fusion | flops 276892672 | bytes 794628 | tf_op jit(solution)/shard_map/while/body/eval_jaxpr/hqk,khd->qhd/dot_general | solution.py:58
  153.4 2.9 fusion.147
  156.3 3.1 %fusion.148 = bf16[4,512,32]{1,2,0:T(8,128)(2,1)S(1)} fusion(bf16[1024,4,32]{0,2,1:T(8,128)(2,1)S(1)} %get-tuple-element.358, f32[4,512]{1,0:T(4,128)S(1)} %fusion.147, bf16[1024,4,32]{0,2,1:T(8,128)(2,1)S(1)} %get-tuple-element.357, bf16[8,512,4,32]{1,3,2,0:T(8,128)(2,1)S(1)} %get-tuple-element.356, s32[]{:T(128)S(6)} %copy.42), kind=kOutput, calls=%fused_computation.8.clone.1 | convolution fusion | flops 276892672 | bytes 794628 | tf_op jit(solution)/shard_map/while/body/eval_jaxpr/hqk,khd->qhd/dot_general | solution.py:58
  160.2 2.9 fusion.147
  163.1 3.1 %fusion.148 = bf16[4,512,32]{1,2,0:T(8,128)(2,1)S(1)} fusion(bf16[1024,4,32]{0,2,1:T(8,128)(2,1)S(1)} %get-tuple-element.358, f32[4,512]{1,0:T(4,128)S(1)} %fusion.147, bf16[1024,4,32]{0,2,1:T(8,128)(2,1)S(1)} %get-tuple-element.357, bf16[8,512,4,32]{1,3,2,0:T(8,128)(2,1)S(1)} %get-tuple-element.356, s32[]{:T(128)S(6)} %copy.42), kind=kOutput, calls=%fused_computation.8.clone.1 | convolution fusion | flops 276892672 | bytes 794628 | tf_op jit(solution)/shard_map/while/body/eval_jaxpr/hqk,khd->qhd/dot_general | solution.py:58
  167.0 2.9 fusion.147
  170.0 3.1 %fusion.148 = bf16[4,512,32]{1,2,0:T(8,128)(2,1)S(1)} fusion(bf16[1024,4,32]{0,2,1:T(8,128)(2,1)S(1)} %get-tuple-element.358, f32[4,512]{1,0:T(4,128)S(1)} %fusion.147, bf16[1024,4,32]{0,2,1:T(8,128)(2,1)S(1)} %get-tuple-element.357, bf16[8,512,4,32]{1,3,2,0:T(8,128)(2,1)S(1)} %get-tuple-element.356, s32[]{:T(128)S(6)} %copy.42), kind=kOutput, calls=%fused_computation.8.clone.1 | convolution fusion | flops 276892672 | bytes 794628 | tf_op jit(solution)/shard_map/while/body/eval_jaxpr/hqk,khd->qhd/dot_general | solution.py:58
  173.8 2.9 fusion.147
  176.8 3.1 %fusion.148 = bf16[4,512,32]{1,2,0:T(8,128)(2,1)S(1)} fusion(bf16[1024,4,32]{0,2,1:T(8,128)(2,1)S(1)} %get-tuple-element.358, f32[4,512]{1,0:T(4,128)S(1)} %fusion.147, bf16[1024,4,32]{0,2,1:T(8,128)(2,1)S(1)} %get-tuple-element.357, bf16[8,512,4,32]{1,3,2,0:T(8,128)(2,1)S(1)} %get-tuple-element.356, s32[]{:T(128)S(6)} %copy.42), kind=kOutput, calls=%fused_computation.8.clone.1 | convolution fusion | flops 276892672 | bytes 794628 | tf_op jit(solution)/shard_map/while/body/eval_jaxpr/hqk,khd->qhd/dot_general | solution.py:58
  180.7 2.9 fusion.147
  183.6 3.1 %fusion.148 = bf16[4,512,32]{1,2,0:T(8,128)(2,1)S(1)} fusion(bf16[1024,4,32]{0,2,1:T(8,128)(2,1)S(1)} %get-tuple-element.358, f32[4,512]{1,0:T(4,128)S(1)} %fusion.147, bf16[1024,4,32]{0,2,1:T(8,128)(2,1)S(1)} %get-tuple-element.357, bf16[8,512,4,32]{1,3,2,0:T(8,128)(2,1)S(1)} %get-tuple-element.356, s32[]{:T(128)S(6)} %copy.42), kind=kOutput, calls=%fused_computation.8.clone.1 | convolution fusion | flops 276892672 | bytes 794628 | tf_op jit(solution)/shard_map/while/body/eval_jaxpr/hqk,khd->qhd/dot_general | solution.py:58
  187.5 2.9 fusion.147
  190.4 3.1 %fusion.148 = bf16[4,512,32]{1,2,0:T(8,128)(2,1)S(1)} fusion(bf16[1024,4,32]{0,2,1:T(8,128)(2,1)S(1)} %get-tuple-element.358, f32[4,512]{1,0:T(4,128)S(1)} %fusion.147, bf16[1024,4,32]{0,2,1:T(8,128)(2,1)S(1)} %get-tuple-element.357, bf16[8,512,4,32]{1,3,2,0:T(8,128)(2,1)S(1)} %get-tuple-element.356, s32[]{:T(128)S(6)} %copy.42), kind=kOutput, calls=%fused_computation.8.clone.1 | convolution fusion | flops 276892672 | bytes 794628 | tf_op jit(solution)/shard_map/while/body/eval_jaxpr/hqk,khd->qhd/dot_general | solution.py:58
  194.3 4.4 %convolution_convert_fusion.1 = bf16[4,1024,512]{2,1,0:T(8,128)(2,1)} fusion(bf16[4,1024,128]{2,1,0:T(8,128)(2,1)} %bitcast.137, bf16[128,512]{1,0:T(8,128)(2,1)S(1)} %copy-done), kind=kOutput, calls=%fused_computation.52 | convolution fusion | flops 538968064 | bytes 5373952 | tf_op jit(solution)/shard_map/dot_general | solution.py:113
  198.8 8.1 %copy.24 = bf16[4,1024,512]{1,0,2:T(4,128)(2,1)} copy(bf16[4,1024,512]{2,1,0:T(8,128)(2,1)} %convolution_convert_fusion.1) | data formatting | bytes 8388608
  206.9 6.4 %copy.30 = bf16[64,8,4,1024]{3,1,2,0:T(8,128)(2,1)} copy(bf16[64,8,4,1024]{3,2,1,0:T(4,128)(2,1)} %bitcast.132) | data formatting | bytes 8388608
  217.6 5.1 %collective-permute-done = bf16[2,1024,128]{2,1,0:T(8,128)(2,1)S(1)} collective-permute-done((bf16[2,1024,128]{2,1,0:T(8,128)(2,1)S(1)}, bf16[2,1024,128]{2,1,0:T(8,128)(2,1)S(1)}, u32[]{:S(2)}, u32[]{:S(2)}) %collective-permute-start) | collective-permute-done | bytes 524320 | tf_op jit(solution)/shard_map/ppermute | solution.py:15
  222.7 4.4 %collective-permute-done.1 = bf16[2,1024,128]{2,1,0:T(8,128)(2,1)S(1)} collective-permute-done((bf16[2,1024,128]{2,1,0:T(8,128)(2,1)S(1)}, bf16[2,1024,128]{2,1,0:T(8,128)(2,1)S(1)}, u32[]{:S(2)}, u32[]{:S(2)}) %collective-permute-start.1) | collective-permute-done | bytes 524320 | tf_op jit(solution)/shard_map/ppermute | solution.py:18
  229.5 34.2 %reduce-scatter.7.cloned.1.call-done = bf16[128,4096]{1,0:T(8,128)(2,1)} async-done(((bf16[512,4096]{1,0:T(8,128)(2,1)}), bf16[128,4096]{1,0:T(8,128)(2,1)}) %reduce-scatter.7.cloned.1.call-update) | async-done | bytes 1048592
  266.5 29.1 %fusion.88 = bf16[4,1024,128]{2,1,0:T(8,128)(2,1)} fusion(f32[8,1028,128]{2,1,0:T(8,128)} %fusion.85, bf16[4,1024,128]{2,1,0:T(8,128)(2,1)S(1)} %copy.25, bf16[4,1024,128]{2,1,0:T(8,128)(2,1)S(1)} %copy-done.3, f32[128]{0:T(128)S(1)} %get-tuple-element.229, f32[128]{0:T(128)S(1)} %get-tuple-element.230, f32[128]{0:T(128)S(1)} %get-tuple-element.207, ...), kind=kLoop, calls=%fused_computation.62 | loop fusion | flops 28311552 | bytes 55587328 | tf_op jit(solution)/shard_map/convert_element_type | solution.py:131
  (79 shorter events, 35.9 us)
Async XLA Ops:
  6.5 187.8 %copy-start = (bf16[128,512]{1,0:T(8,128)(2,1)S(1)}, bf16[128,512]{1,0:T(8,128)(2,1)}, u32[]{:S(2)}) copy-start(bf16[128,512]{1,0:T(8,128)(2,1)} %param.21) | copy-start | bytes 393220
  6.5 57.8 %all-gather.2.cloned.1.call-start = ((), (), s32[]{:S(2)}) async-start(), calls=%async_computation.2 | async-start | bytes 5242880 | tf_op jit(solution)/shard_map/all_gather | solution.py:68
  7.3 94.0 %reduce-scatter.5.cloned.1.call-start = ((), (), s32[]{:S(2)}) async-start(), calls=%async_computation.3 | async-start | bytes 327680 | tf_op jit(solution)/shard_map/reduce_scatter | solution.py:96
  64.4 3.4 %copy-start.1 = (bf16[4,1024,512]{2,1,0:T(8,128)(2,1)S(1)}, bf16[4,1024,512]{2,1,0:T(8,128)(2,1)}, u32[]{:S(2)}) copy-start(bf16[4,1024,512]{2,1,0:T(8,128)(2,1)} %all-gather.2.cloned.1.call-done) | copy-start | bytes 12582916
  67.8 1.6 copy-start.9
  71.1 1.9 copy-start.2
  73.0 0.7 copy-start.8
  73.7 7.5 %copy-start.4 = (bf16[512,128]{1,0:T(8,128)(2,1)S(1)}, bf16[512,128]{1,0:T(8,128)(2,1)}, u32[]{:S(2)}) copy-start(bf16[512,128]{1,0:T(8,128)(2,1)} %param.18) | copy-start | bytes 393220
  81.1 182.5 %reduce-scatter.7.cloned.1.call-start = ((), (), s32[]{:S(2)}) async-start(), calls=%async_computation.4 | async-start | bytes 5242880
  85.2 25.3 %copy-start.5 = (bf16[512,128]{1,0:T(8,128)(2,1)S(1)}, bf16[512,128]{1,0:T(8,128)(2,1)}, u32[]{:S(2)}) copy-start(bf16[512,128]{1,0:T(8,128)(2,1)} %param.20) | copy-start | bytes 393220
  85.2 25.6 %copy-start.6 = (bf16[512,128]{1,0:T(8,128)(2,1)S(1)}, bf16[512,128]{1,0:T(8,128)(2,1)}, u32[]{:S(2)}) copy-start(bf16[512,128]{1,0:T(8,128)(2,1)} %param.19) | copy-start | bytes 393220
  213.4 4.2 %copy-start.7 = (f32[25,128]{1,0:T(8,128)S(1)}, f32[25,128]{1,0:T(8,128)}, u32[]{:S(2)}) copy-start(f32[25,128]{1,0:T(8,128)} %param.22) | copy-start | bytes 38404
  214.7 8.0 %collective-permute-start = (bf16[2,1024,128]{2,1,0:T(8,128)(2,1)S(1)}, bf16[2,1024,128]{2,1,0:T(8,128)(2,1)S(1)}, u32[]{:S(2)}, u32[]{:S(2)}) collective-permute-start(bf16[2,1024,128]{2,1,0:T(8,128)(2,1)S(1)} %get-tuple-element.204), channel_id=1, source_target_pairs={{0,8},{8,16},{16,24},{1,9},{9,17},{17,25},{2,10},{10,18},{18,26},{... | collective-permute-start | bytes 1572872 | tf_op jit(solution)/shard_map/ppermute | solution.py:15
  216.0 11.1 %collective-permute-start.1 = (bf16[2,1024,128]{2,1,0:T(8,128)(2,1)S(1)}, bf16[2,1024,128]{2,1,0:T(8,128)(2,1)S(1)}, u32[]{:S(2)}, u32[]{:S(2)}) collective-permute-start(bf16[2,1024,128]{2,1,0:T(8,128)(2,1)S(1)} %get-tuple-element.205), channel_id=1, source_target_pairs={{8,0},{16,8},{24,16},{9,1},{17,9},{25,17},{10,2},{18,10},{26,18},{... | collective-permute-start | bytes 1572872 | tf_op jit(solution)/shard_map/ppermute | solution.py:18
  229.5 37.0 %copy-start.3 = (bf16[4,1024,128]{2,1,0:T(8,128)(2,1)S(1)}, bf16[4,1024,128]{2,1,0:T(8,128)(2,1)}, u32[]{:S(2)}) copy-start(bf16[4,1024,128]{2,1,0:T(8,128)(2,1)} %param.14) | copy-start | bytes 3145732
Sparse Core Ops, SparseCore 0:
  9.2 55.1 all-gather.1
  81.2 19.9 reduce-scatter.4
  213.5 50.1 reduce-scatter.6
where the time goes:
time: 303 us; the launch traced here: 302 us
  waiting for transfers between devices  113 us (37%)
  matrix products  63.1 us (21%)
  other arithmetic  42 us (14%)
  blocking collectives  37.5 us (12%)
  local copies, waits for them, and re-layouts  29.8 us (10%)
  between operations  13.4 us (4%)
    all_gather x1, waiting for transfers between devices, shards(): whole = lax.all_gather(tokens, 'head', axis=2, tiled=True)  53.4 us
    unnamed x4, waiting for transfers between devices  34.9 us
    convert_element_type x1, other arithmetic, shards(): return total.astype(jnp.bfloat16)  29.1 us
    dot_general x8, matrix products, one_block(): jnp.einsum('hqk,khd->qhd', probs, value_heads, preferred_element_type=jnp...  24.7 us
    sub x8, matrix products, one_block(): expo = jnp.exp(scores - top)  23.4 us
    unnamed x25, local copies, waits for them, and re-layouts  20.7 us
    reduce_scatter x1, waiting for transfers between devices, shards(): lax.psum_scatter(sample_points(normed_here, col_table, row_table, share_r...  15.3 us
    all_gather x1, blocking collectives, shards(): lax.all_gather(key_share, 'band', axis=0, tiled=True)  14.3 us
  transfers between devices with their start and end apart: 5, of which 5 were waited for; matrix products, arithmetic and copies ran while one was open for 4% of the time, Pallas kernels for 0%

commit v1 on v0

v1 whole, which is shorter than its diff:
```python
import functools
import math

import jax
import jax.numpy as jnp
from jax import lax
from jax.experimental import pallas as pl
from jax.experimental.pallas import tpu as pltpu
from jax.sharding import PartitionSpec as P

HEADS = 16
KER = 5
EPS = 1e-05
BF = jnp.bfloat16
F32 = jnp.float32
VM = pl.BlockSpec(memory_space=pltpu.VMEM)


def params(**more):
    return pltpu.CompilerParams(vmem_limit_bytes=60 * 1024 * 1024, **more)


def dot(a, b, dims=((1,), (0,))):
    return lax.dot_general(a, b, (dims, ((), ())), preferred_element_type=F32)


def shift(me, off, count):
    return lax.rem(me + off, count)


def remote(src, dst, send, recv, where):
    return pltpu.make_async_remote_copy(
        src_ref=src,
        dst_ref=dst,
        send_sem=send,
        recv_sem=recv,
        device_id=where,
        device_id_type=pl.DeviceIdType.MESH,
    )


def greet(places):
    barrier = pltpu.get_barrier_semaphore()
    for where in places:
        pl.semaphore_signal(barrier, inc=1, device_id=where, device_id_type=pl.DeviceIdType.MESH)
    pl.semaphore_wait(barrier, len(places))


def stats_kernel(x_ref, out_ref):
    x = x_ref[0]
    channels = x.shape[1]
    part = 1.0 / channels
    mean = dot(x, jnp.full((channels, channels), part, BF))
    square = jnp.square(x.astype(F32) - mean)
    high = square.astype(BF)
    low = (square - high.astype(F32)).astype(BF)
    ones = jnp.ones((8, channels), BF)
    rows = ((1,), (1,))
    mean_row = dot(jnp.full((8, channels), part, BF), x, rows)
    spread_row = dot(ones, high, rows) + dot(ones, low, rows)
    out_ref[0:1, :] = mean_row[0:1]
    out_ref[1:2, :] = spread_row[0:1]


def local_stats(tokens):
    band_rows, columns, channels = tokens.shape
    return pl.pallas_call(
        stats_kernel,
        grid=(band_rows,),
        in_specs=[pl.BlockSpec((1, columns, channels), lambda i: (i, 0, 0))],
        out_specs=pl.BlockSpec((2, columns), lambda i: (0, i)),
        out_shape=jax.ShapeDtypeStruct((2, band_rows * columns), F32),
        compiler_params=params(),
        name="local_stats",
    )(tokens)


def first_kernel(n_head, n_band, margin, *refs):
    tok, stat, wq, wk, wv, wo = refs[:6]
    xs, stats, halo, gq, gk, gv, go = refs[6:13]
    send, recv, hsend, hrecv, dsend, drecv = refs[13:]
    head, band, dp = (lax.axis_index(name) for name in ("head", "band", "dp"))
    places = [{"head": shift(head, off, n_head)} for off in range(1, n_head)]
    places += [{"band": shift(band, 1, n_band)}, {"band": shift(band, n_band - 1, n_band)}]
    places += [{"dp": 1 - dp}]
    greet(places)
    rows = tok.shape[0]
    per_head = rows // n_head
    others = range(1, n_head)
    copies = {}
    for off in others:
        to = shift(head, off, n_head)
        pairs = [(stat, stats.at[head]), (tok.at[pl.ds(to * per_head, per_head)], xs.at[head])]
        for k, (src, dst) in enumerate(pairs):
            copies[k, off] = remote(src, dst, send.at[k, off - 1], recv.at[k, off - 1], {"head": to})
            copies[k, off].start()
    up = remote(
        tok.at[pl.ds(rows - margin, margin)], halo.at[0], hsend.at[0], hrecv.at[0],
        {"band": shift(band, 1, n_band)},
    )
    down = remote(
        tok.at[pl.ds(0, margin)], halo.at[1], hsend.at[1], hrecv.at[1],
        {"band": shift(band, n_band - 1, n_band)},
    )

    @pl.when(band < n_band - 1)
    def _():
        up.start()

    @pl.when(band > 0)
    def _():
        down.start()

    weights = [(wq, gq), (wk, gk), (wv, gv), (wo, go)]
    for off in others:
        to = shift(head, off, n_head)
        for k, (src, dst) in enumerate(weights):
            c = remote(src.at[dp], dst.at[dp, head], send.at[k + 2, off - 1], recv.at[k + 2, off - 1], {"head": to})
            copies[k + 2, off] = c
            c.start()
    xs[head] = tok[pl.ds(head * per_head, per_head)]
    stats[head] = stat[...]
    halves = []
    for src, dst in weights:
        dst[dp, head] = src[dp]
        dst[1 - dp, head] = src[1 - dp]
    for off in others:
        back = shift(head, n_head - off, n_head)
        for k, (src, dst) in enumerate(weights):
            copies[k + 2, off].wait_recv()
            c = remote(
                dst.at[dp, back], dst.at[dp, back], dsend.at[k, off - 1], drecv.at[k, off - 1],
                {"dp": 1 - dp},
            )
            c.start()
            halves.append(c)
    for off in others:
        for k in range(2):
            copies[k, off].wait()
        for k in range(4):
            copies[k + 2, off].wait_send()
    for c in halves:
        c.wait()

    @pl.when(band < n_band - 1)
    def _():
        up.wait_send()
        down.wait_recv()

    @pl.when(band > 0)
    def _():
        down.wait_send()
        up.wait_recv()


def first_exchange(tokens, stat, wq, wk, wv, wo, n_head, n_band):
    band_rows, columns, channels = tokens.shape
    margin = KER // 2
    halves = [w.reshape(2, w.shape[0] // 2, w.shape[1]) for w in (wq, wk, wv, wo)]
    outs = [
        jax.ShapeDtypeStruct((n_head, band_rows // n_head, columns, channels), tokens.dtype),
        jax.ShapeDtypeStruct((n_head,) + stat.shape, stat.dtype),
        jax.ShapeDtypeStruct((2, margin, columns, channels), tokens.dtype),
    ] + [jax.ShapeDtypeStruct((2, n_head) + w.shape[1:], w.dtype) for w in halves]
    sems = [pltpu.SemaphoreType.DMA((6, n_head - 1))] * 2
    sems += [pltpu.SemaphoreType.DMA((2,))] * 2
    sems += [pltpu.SemaphoreType.DMA((4, n_head - 1))] * 2
    return pl.pallas_call(
        functools.partial(first_kernel, n_head, n_band, margin),
        out_shape=outs,
        in_specs=[VM] * 6,
        out_specs=[VM] * 7,
        scratch_shapes=sems,
        compiler_params=params(collective_id=0, has_side_effects=True),
        name="first_exchange",
    )(tokens, stat, *halves)


def prepare_kernel(factor, n_head, n_band, tok, xs, stats, gain, cr, cc, fr, gq, normed, query, part, edge, wide, weight, comb, turned):
    rows, columns, channels = tok.shape
    head, band = lax.axis_index("head"), lax.axis_index("band")
    mean = stats[0, 0:1]
    for i in range(1, n_head):
        mean = mean + stats[i, 0:1]
    mean = mean * (1.0 / n_head)
    total = jnp.zeros_like(mean)
    for i in range(n_head):
        total = total + stats[i, 1:2] + channels * jnp.square(stats[i, 0:1] - mean)
    inv = lax.rsqrt(total * (1.0 / (n_head * channels)) + EPS)
    comb[...] = jnp.zeros_like(comb)
    comb[0:1, :] = mean
    comb[1:2, :] = inv
    margin = edge.shape[2] // columns
    edge[0] = comb[0:2, (rows - margin) * columns :]
    edge[1] = comb[0:2, : margin * columns]
    for r in range(rows):
        col = comb[:, r * columns : (r + 1) * columns].T
        value = ((tok[r].astype(F32) - col[:, 0:1]) * col[:, 1:2] * gain[head]).astype(BF)
        normed[r] = value
        turned[r * channels : (r + 1) * channels, :] = value.T
    per = xs.shape[1] * columns
    for r in range(xs.shape[1]):
        begin = pl.multiple_of(head * per + r * columns, 128)
        col = comb[:, pl.ds(begin, columns)].T
        for i in range(n_head):
            value = (xs[i, r].astype(F32) - col[:, 0:1]) * col[:, 1:2] * gain[i]
            wide[r * columns : (r + 1) * columns, i * channels : (i + 1) * channels] = value.astype(BF)
    half = gq.shape[2]
    for a in range(2):
        for i in range(n_head):
            weight[a * half : (a + 1) * half, i * channels : (i + 1) * channels] = gq[a, i]

    @pl.loop(0, per // 256)
    def _(step):
        at = pl.ds(pl.multiple_of(step * 256, 256), 256)
        query[at, :] = (dot(wide[at, :], weight[...]) * factor).astype(BF)

    left = (1.0 - fr[1:2]).astype(BF).astype(F32)
    right = fr[1:2].astype(BF).astype(F32)
    top = (1.0 - fr[0:1]).astype(BF).astype(F32)
    bottom = fr[0:1].astype(BF).astype(F32)
    points = cc.shape[1]
    share = channels // n_band
    block = 256

    for begin in range(0, points, block):
        at = slice(begin, begin + block)
        spot = lax.broadcasted_iota(jnp.int32, (columns, block), 0)
        table = jnp.where(
            spot == cc[:, at], left[:, at], jnp.where(spot == cc[:, at] + 1, right[:, at], 0.0)
        ).astype(BF)
        inner = dot(turned[...], table)
        total = jnp.zeros((channels, block), F32)
        for r in range(rows):
            row = band * rows + r
            w = jnp.where(cr[:, at] == row, top[:, at], 0.0) + jnp.where(
                cr[:, at] + 1 == row, bottom[:, at], 0.0
            )
            total = total + w * inner[r * channels : (r + 1) * channels]
        for b in range(n_band):
            part[b, :, at] = total[b * share : (b + 1) * share].astype(BF)


def prepare(tokens, xs, stats, gain, cr, cc, fr, gq, n_head, n_band, factor):
    rows, columns, channels = tokens.shape
    points = cc.shape[1]
    per = xs.shape[1] * columns
    width = n_head * channels
    margin = KER // 2
    return pl.pallas_call(
        functools.partial(prepare_kernel, factor, n_head, n_band),
        out_shape=[
            jax.ShapeDtypeStruct(tokens.shape, BF),
            jax.ShapeDtypeStruct((per, width), BF),
            jax.ShapeDtypeStruct((n_band, channels // n_band, points), BF),
            jax.ShapeDtypeStruct((2, 2, margin * columns), F32),
        ],
        in_specs=[VM] * 8,
        out_specs=[VM] * 4,
        scratch_shapes=[
            pltpu.VMEM((per, width), BF),
            pltpu.VMEM((width, width), BF),
            pltpu.VMEM((8, rows * columns), F32),
            pltpu.VMEM((rows * channels, columns), BF),
        ],
        compiler_params=params(),
        name="prepare",
    )(tokens, xs, stats, gain, cr, cc, fr, gq)


def second_kernel(n_head, n_band, part, edge, whole, rim, landed, bsend, brecv, esend, erecv, zsend, zrecv, hsend, hrecv):
    head, band = lax.axis_index("head"), lax.axis_index("band")
    places = [{"head": shift(head, off, n_head)} for off in range(1, n_head)]
    places += [{"band": shift(band, off, n_band)} for off in range(1, n_band)]
    greet(places)
    bands, heads = range(1, n_band), range(1, n_head)
    parts = []
    for off in bands:
        to = shift(band, off, n_band)
        c = remote(part.at[to], landed.at[off - 1], bsend.at[off - 1], brecv.at[off - 1], {"band": to})
        c.start()
        parts.append(c)
    up = remote(edge.at[0], rim.at[0], esend.at[0], erecv.at[0], {"band": shift(band, 1, n_band)})
    down = remote(
        edge.at[1], rim.at[1], esend.at[1], erecv.at[1], {"band": shift(band, n_band - 1, n_band)}
    )
    up.start()
    down.start()
    total = part[band].astype(F32)
    for off in bands:
        parts[off - 1].wait_recv()
        total = total + landed[off - 1].astype(F32)
    whole[band, head] = total.astype(BF)
    along, across = [], []
    for off in bands:
        c = remote(
            whole.at[band, head], whole.at[band, head], zsend.at[off - 1], zrecv.at[off - 1],
            {"band": shift(band, off, n_band)},
        )
        c.start()
        along.append(c)
    for step in range(n_band):
        source = shift(band, n_band - step, n_band)
        if step:
            along[step - 1].wait_recv()
        for off in heads:
            c = remote(
                whole.at[source, head], whole.at[source, head], hsend.at[step, off - 1],
                hrecv.at[step, off - 1], {"head": shift(head, off, n_head)},
            )
            c.start()
            across.append(c)
    for c in across:
        c.wait()
    for c in along + parts:
        c.wait_send()
    up.wait()
    down.wait()


def second_exchange(part, edge, n_head, n_band):
    sem = pltpu.SemaphoreType.DMA
    return pl.pallas_call(
        functools.partial(second_kernel, n_head, n_band),
        out_shape=[
            jax.ShapeDtypeStruct((n_band, n_head) + part.shape[1:], BF),
            jax.ShapeDtypeStruct(edge.shape, F32),
        ],
        in_specs=[VM] * 2,
        out_specs=[VM] * 2,
        scratch_shapes=[pltpu.VMEM((n_band - 1,) + part.shape[1:], BF)]
        + [sem((n_band - 1,))] * 2
        + [sem((2,))] * 2
        + [sem((n_band - 1,))] * 2
        + [sem((n_band, n_head - 1))] * 2,
        compiler_params=params(collective_id=1, has_side_effects=True),
        name="second_exchange",
    )(part, edge)


def attend_kernel(size, query, samples, gk, gv, go, out, sampled, turned, keys, values, weight, attended):
    n_band, n_head, share, points = samples.shape
    channels = share * n_band
    half = gk.shape[2]
    group = channels // size
    for b in range(n_band):
        for i in range(n_head):
            at = i * channels + b * share
            sampled[at : at + share, :] = samples[b, i]
    turned[...] = sampled[...].T
    low = go.shape[2]
    for a in range(2):
        for i in range(n_head):
            at = i * channels + a * low
            weight[at : at + low, :] = go[a, i]

    @pl.loop(0, n_head)
    def _(i):
        flip = ((0,), (0,))
        key = dot(gk[0, i], sampled[0:half, :], flip) + dot(gk[1, i], sampled[half:, :], flip)
        value = dot(turned[:, 0:half], gv[0, i]) + dot(turned[:, half:], gv[1, i])
        key_spot = lax.broadcasted_iota(jnp.int32, key.shape, 0)
        value_spot = lax.broadcasted_iota(jnp.int32, value.shape, 1)
        for j in range(group):
            low_end, high_end = j * size, (j + 1) * size
            keep = (key_spot >= low_end) & (key_spot < high_end)
            keys[i * group + j] = jnp.where(keep, key, 0.0).astype(BF)
            keep = (value_spot >= low_end) & (value_spot < high_end)
            values[i * group + j, :, 0:channels] = jnp.where(keep, value, 0.0).astype(BF)
            values[i * group + j, :, channels:] = jnp.ones((points, channels), BF)

    block = attended.shape[0]

    @pl.loop(0, query.shape[0] // block)
    def _(step):
        at = pl.ds(pl.multiple_of(step * block, block), block)

        @pl.loop(0, n_head)
        def _(i):
            lanes = pl.ds(pl.multiple_of(i * channels, channels), channels)
            q = query[at, lanes]
            total = jnp.zeros((block, channels), F32)
            for j in range(group):
                score = dot(q, keys[i * group + j])
                top = jnp.max(score, axis=1, keepdims=True)
                prob = jnp.exp2(score - top).astype(BF)
                both = dot(prob, values[i * group + j])
                total = total + both[:, 0:channels] / both[:, channels:]
            attended[:, lanes] = total.astype(BF)

        result = dot(attended[...], weight[...])
        for i in range(n_head):
            out[i, at, :] = result[:, i * channels : (i + 1) * channels].astype(BF)


def attend(query, samples, gk, gv, go):
    n_band, n_head, share, points = samples.shape
    count, width = query.shape
    channels = width // n_head
    return pl.pallas_call(
        functools.partial(attend_kernel, width // HEADS),
        out_shape=jax.ShapeDtypeStruct((n_head, count, channels), BF),
        in_specs=[VM] * 5,
        out_specs=VM,
        scratch_shapes=[
            pltpu.VMEM((width, points), BF),
            pltpu.VMEM((points, width), BF),
            pltpu.VMEM((HEADS, channels, points), BF),
            pltpu.VMEM((HEADS, points, 2 * channels), BF),
            pltpu.VMEM((width, width), BF),
            pltpu.VMEM((256, width), BF),
        ],
        compiler_params=params(),
        name="attend",
    )(query, samples, gk, gv, go)


def third_kernel(n_head, mine, out, send, recv):
    head = lax.axis_index("head")
    greet([{"head": shift(head, off, n_head)} for off in range(1, n_head)])
    copies = []
    for off in range(1, n_head):
        to = shift(head, off, n_head)
        c = remote(mine.at[to], out.at[head], send.at[off - 1], recv.at[off - 1], {"head": to})
        c.start()
        copies.append(c)
    out[head] = mine[head]
    for c in copies:
        c.wait()


def third_exchange(mine, n_head):
    return pl.pallas_call(
        functools.partial(third_kernel, n_head),
        out_shape=jax.ShapeDtypeStruct(mine.shape, BF),
        in_specs=[VM],
        out_specs=VM,
        scratch_shapes=[pltpu.SemaphoreType.DMA((n_head - 1,))] * 2,
        compiler_params=params(collective_id=2, has_side_effects=True),
        name="third_exchange",
    )(mine)


def mix_kernel(n_band, tok, normed, halo, rim, gain, taps, projected, out, padded, comb):
    rows, columns, channels = tok.shape
    margin = KER // 2
    head, band = lax.axis_index("head"), lax.axis_index("band")
    edge = 8
    padded[:, 0:edge, :] = jnp.zeros((rows + 2 * margin, edge, channels), F32)
    padded[:, edge + columns :, :] = jnp.zeros((rows + 2 * margin, edge, channels), F32)
    for r in range(rows):
        padded[margin + r, edge : edge + columns, :] = normed[r].astype(F32)
    for side in range(2):
        comb[...] = jnp.zeros_like(comb)
        comb[0:2, :] = rim[side]
        there = band > 0 if side == 0 else band < n_band - 1
        for r in range(margin):
            col = comb[:, r * columns : (r + 1) * columns].T
            value = (halo[side, r].astype(F32) - col[:, 0:1]) * col[:, 1:2] * gain[head]
            value = jnp.where(there, value.astype(BF).astype(F32), 0.0)
            padded[side * (margin + rows) + r, edge : edge + columns, :] = value
    block = 64

    @pl.loop(0, rows)
    def _(r):
        @pl.loop(0, columns // block)
        def _(step):
            begin = pl.multiple_of(step * block, block)
            at = pl.ds(begin, block)
            total = tok[r, at, :].astype(F32) + projected[r, at, :].astype(F32)
            for a in range(KER):
                for b in range(KER):
                    total = total + taps[a * KER + b : a * KER + b + 1, :] * padded[
                        r + a, pl.ds(begin + (edge - margin + b), block), :
                    ]
            out[r, at, :] = total.astype(BF)


def mix(tokens, normed, halo, rim, gain, taps, projected, n_band):
    rows, columns, channels = tokens.shape
    margin = KER // 2
    return pl.pallas_call(
        functools.partial(mix_kernel, n_band),
        out_shape=jax.ShapeDtypeStruct(tokens.shape, BF),
        in_specs=[VM] * 7,
        out_specs=VM,
        scratch_shapes=[
            pltpu.VMEM((rows + 2 * margin, columns + 16, channels), F32),
            pltpu.VMEM((8, margin * columns), F32),
        ],
        compiler_params=params(),
        name="mix",
    )(tokens, normed, halo, rim, gain, taps, projected)


def shards(
    tokens, corner_row, corner_col, fraction, w_query, w_key, w_value, w_out, conv_kernel, norm_gain
):
    n_head, n_band = lax.axis_size("head"), lax.axis_size("band")
    channels = tokens.shape[2]
    width = n_head * channels
    factor = math.log2(math.e) / math.sqrt(width // HEADS)
    gain = norm_gain.reshape(n_head, 1, channels)
    stat = local_stats(tokens)
    xs, stats, halo, gq, gk, gv, go = first_exchange(
        tokens, stat, w_query, w_key, w_value, w_out, n_head, n_band
    )
    normed, query, part, edge = prepare(
        tokens, xs, stats, gain, corner_row[None], corner_col[None], fraction, gq,
        n_head, n_band, factor,
    )
    samples, rim = second_exchange(part, edge, n_head, n_band)
    mine = attend(query, samples, gk, gv, go)
    projected = third_exchange(mine, n_head).reshape(tokens.shape)
    return mix(tokens, normed, halo, rim, gain, conv_kernel, projected, n_band)


def solution(mesh):
    return jax.shard_map(
        shards,
        mesh=mesh,
        in_specs=(
            P(("dp", "band"), None, "head"),
            P("dp"),
            P("dp"),
            P(None, "dp"),
            P(None, "head"),
            P(None, "head"),
            P(None, "head"),
            P("head", None),
            P(None, "head"),
            P(),
        ),
        out_specs=P(("dp", "band"), None, "head"),
        check_vma=False,
    )
```

time: 303 us -> 135 us (0.45)
  Pallas kernels: 0 us -> 134 us
  waiting for transfers between devices: 113 us -> 0 us
  matrix products: 63.1 us -> 0 us
  other arithmetic: 42 us -> 0 us
  blocking collectives: 37.5 us -> 0 us
  local copies, waits for them, and re-layouts: 29.8 us -> 0 us
  between operations: 13.4 us -> 0.03 us
    pallas_call x0 -> x7, Pallas kernels: none -> 134 us  [the longest x1 37.5 us: attend(): pl.pallas_call(functools.partial(attend_kernel, width // HEADS), out_shap...]
    all_gather x1 -> x0, waiting for transfers between devices: 53.4 us -> none  [shards(): whole = lax.all_gather(tokens, 'head', axis=2, tiled=True)]
    dot_general x16 -> x0, matrix products: 39.7 us -> none  [the longest x8 24.7 us: one_block(): jnp.einsum('hqk,khd->qhd', probs, value_heads, preferred_element_type=jnp...]
    all_gather x3 -> x0, blocking collectives: 37.5 us -> none  [the longest x1 14.3 us: shards(): lax.all_gather(key_share, 'band', axis=0, tiled=True)]
    convert_element_type x6 -> x0, other arithmetic: 35.3 us -> none  [the longest x1 29.1 us: shards(): return total.astype(jnp.bfloat16)]
    unnamed x4 -> x0, waiting for transfers between devices: 34.9 us -> none
    sub x8 -> x0, matrix products: 23.4 us -> none  [one_block(): expo = jnp.exp(scores - top)]
    unnamed x25 -> x0, local copies, waits for them, and re-layouts: 20.7 us -> none
  transfers between devices with their start and end apart: 5 -> 0, of which waited for: 5 -> 0; matrix products, arithmetic and copies ran while one was open for 4% -> 0% of each run, Pallas kernels for 0% -> 0%
where the time goes in v1:
time: 135 us; the launch traced here: 134 us
  Pallas kernels  134 us (99%)
    pallas_call x1, Pallas kernels, attend(): pl.pallas_call(functools.partial(attend_kernel, width // HEADS), out_shap...  37.5 us
    pallas_call x1, Pallas kernels, first_exchange(): pl.pallas_call(functools.partial(first_kernel, n_head, n_band, margin), o...  36.1 us
    pallas_call x1, Pallas kernels, second_exchange(): pl.pallas_call(functools.partial(second_kernel, n_head, n_band), out_shap...  24.6 us
    pallas_call x1, Pallas kernels, third_exchange(): pl.pallas_call(functools.partial(third_kernel, n_head), out_shape=jax.Sha...  14.1 us
    pallas_call x1, Pallas kernels, mix(): pl.pallas_call(functools.partial(mix_kernel, n_band), out_shape=jax.Shape...  9.54 us
    pallas_call x1, Pallas kernels, prepare(): pl.pallas_call(functools.partial(prepare_kernel, factor, n_head, n_band),...  8.07 us
    pallas_call x1, Pallas kernels, local_stats(): pl.pallas_call(stats_kernel, grid=(band_rows,), in_specs=[pl.BlockSpec((1...  4.07 us

profile of v1, /device:TPU:0, one launch (start us, length us, event | category | flops | bytes accessed | tf_op | source)
XLA Modules:
  0.0 134.1 jit_solution(17932835631003402154)
XLA Ops:
  0.0 4.1 %local_stats.1.refs_1_ = f32[2,4096]{1,0:T(2,128)} custom-call(bf16[4,1024,128]{2,1,0:T(8,128)(2,1)} %tok.3), custom_call_target="tpu_custom_call" | custom-call | tf_op jit(solution)/shard_map/local_stats/pallas_call | solution.py:67
  4.1 36.1 %first_exchange.1 = (bf16[4,1,1024,128]{3,2,1,0:T(8,128)(2,1)}, f32[4,2,4096]{2,1,0:T(2,128)}, bf16[2,2,1024,128]{3,2,1,0:T(8,128)(2,1)}, bf16[2,4,256,128]{3,2,...) custom-call(bf16[4,1024,128]{2,1,0:T(8,128)(2,1)} %tok.3, ...), custom_call_target="tpu_custom_call" | custom-call | tf_op jit(solution)/shard_map/first_exchange/pallas_call | solution.py:168
  40.2 8.1 %prepare.1 = (bf16[4,1024,128]{2,1,0:T(8,128)(2,1)}, bf16[1024,512]{1,0:T(8,128)(2,1)}, bf16[4,32,1024]{2,1,0:T(8,128)(2,1)}, f32[2,2,2048]{2,1,0:T(2,128)}) custom-call(bf16[4,1024,128]{2,1,0:T(8,128)(2,1)} %tok.3, bf16[4,1,1024,128]{3,2,1,0:T(8,128)(2,1)} %get-tuple-element.18.xs, f32[4,2,4096]{2,1,0:T(2,128)} %get-tuple-element.19.stats, ...), custom_call_target="tpu_custom_call" | custom-call | tf_op jit(solution)/shard_map/prepare/pallas_call | solution.py:250
  48.2 24.6 %second_exchange.1 = (bf16[4,4,32,1024]{3,2,1,0:T(8,128)(2,1)}, f32[2,2,2048]{2,1,0:T(2,128)}) custom-call(bf16[4,32,1024]{2,1,0:T(8,128)(2,1)} %get-tuple-element.23.part, f32[2,2,2048]{2,1,0:T(2,128)} %get-tuple-element.24.edge), custom_call_target="tpu_custom_call" | custom-call | tf_op jit(solution)/shard_map/second_exchange/pallas_call | solution.py:323
  72.8 37.5 %attend.1.mine = bf16[4,1024,128]{2,1,0:T(8,128)(2,1)} custom-call(bf16[1024,512]{1,0:T(8,128)(2,1)} %get-tuple-element.26.query, bf16[4,4,32,1024]{3,2,1,0:T(8,128)(2,1)} %get-tuple-element.27.samples, bf16[2,4,256,128]{3,2,1,0:T(8,128)(2,1)} %get-tuple-element.28.gk, bf16[2,4,256,128]{3,2,1,0:T(8,128)(2,1)} %get-tuple-element.29.gv, ...), custom_call_target="tpu_custom_call" | custom-call | tf_op jit(solution)/shard_map/attend/pallas_call | solution.py:400
  110.4 14.1 %third_exchange.1.projected = bf16[4,1024,128]{2,1,0:T(8,128)(2,1)} custom-call(bf16[4,1024,128]{2,1,0:T(8,128)(2,1)} %attend.1.mine), custom_call_target="tpu_custom_call" | custom-call | tf_op jit(solution)/shard_map/third_exchange/pallas_call | solution.py:433
  124.5 9.5 %mix.1 = bf16[4,1024,128]{2,1,0:T(8,128)(2,1)} custom-call(bf16[4,1024,128]{2,1,0:T(8,128)(2,1)} %tok.3, bf16[4,1024,128]{2,1,0:T(8,128)(2,1)} %get-tuple-element.21.normed, bf16[2,2,1024,128]{3,2,1,0:T(8,128)(2,1)} %get-tuple-element.22.halo, f32[2,2,2048]{2,1,0:T(2,128)} %get-tuple-element.25.rim, f32[4,1,128]{2,1,0:T(1,128)} %bitcast.12, f32[25,128]{1,0:T(8,128)} %taps.1, ...), custom_call_target="tpu_custom_call" | custom-call | tf_op jit(solution)/shard_map/mix/pallas_call | solution.py:482

commit v2 on v1

v2 whole, which is shorter than its diff:
```python
import functools
import math

import jax
import jax.numpy as jnp
from jax import lax
from jax.experimental import pallas as pl
from jax.experimental.pallas import tpu as pltpu
from jax.sharding import PartitionSpec as P

HEADS = 16
KER = 5
EPS = 1e-05
BF = jnp.bfloat16
F32 = jnp.float32
VM = pl.BlockSpec(memory_space=pltpu.VMEM)


def params(**more):
    return pltpu.CompilerParams(vmem_limit_bytes=60 * 1024 * 1024, **more)


def dot(a, b, dims=((1,), (0,))):
    return lax.dot_general(a, b, (dims, ((), ())), preferred_element_type=F32)


def shift(me, off, count):
    return lax.rem(me + off, count)


def remote(src, dst, send, recv, where):
    return pltpu.make_async_remote_copy(
        src_ref=src,
        dst_ref=dst,
        send_sem=send,
        recv_sem=recv,
        device_id=where,
        device_id_type=pl.DeviceIdType.MESH,
    )


def greet(places):
    barrier = pltpu.get_barrier_semaphore()
    for where in places:
        pl.semaphore_signal(barrier, inc=1, device_id=where, device_id_type=pl.DeviceIdType.MESH)
    pl.semaphore_wait(barrier, len(places))


def gather_start(pairs, head, dp, n_head, send, recv):
    copies = {}
    for off in range(1, n_head):
        to = shift(head, off, n_head)
        for k, (src, dst) in enumerate(pairs):
            c = remote(src.at[dp], dst.at[dp, head], send.at[k, off - 1], recv.at[k, off - 1], {"head": to})
            c.start()
            copies[k, off] = c
    for src, dst in pairs:
        dst[dp, head] = src[dp]
        dst[1 - dp, head] = src[1 - dp]
    return copies


def gather_relay(pairs, copies, head, dp, n_head, send, recv):
    halves = []
    for off in range(1, n_head):
        back = shift(head, n_head - off, n_head)
        for k, (src, dst) in enumerate(pairs):
            copies[k, off].wait_recv()
            c = remote(dst.at[dp, back], dst.at[dp, back], send.at[k, off - 1], recv.at[k, off - 1], {"dp": 1 - dp})
            c.start()
            halves.append(c)
    return halves


def gather_finish(copies, halves):
    for c in copies.values():
        c.wait_send()
    for c in halves:
        c.wait()


def gather_sems(count, n_head):
    return [pltpu.SemaphoreType.DMA((count, n_head - 1))] * 4


def halved(w):
    return w.reshape(2, w.shape[0] // 2, w.shape[1])


def stats_row(x):
    channels = x.shape[1]
    part = 1.0 / channels
    mean = dot(x, jnp.full((channels, channels), part, BF))
    square = jnp.square(x.astype(F32) - mean)
    high = square.astype(BF)
    low = (square - high.astype(F32)).astype(BF)
    ones = jnp.ones((8, channels), BF)
    rows = ((1,), (1,))
    mean_row = dot(jnp.full((8, channels), part, BF), x, rows)
    spread_row = dot(ones, high, rows) + dot(ones, low, rows)
    return mean_row[0:1], spread_row[0:1]


def first_kernel(n_head, n_band, margin, tok, xs, stats, halo, stat, send, recv, hsend, hrecv):
    head, band = lax.axis_index("head"), lax.axis_index("band")
    places = [{"head": shift(head, off, n_head)} for off in range(1, n_head)]
    places += [{"band": shift(band, 1, n_band)}, {"band": shift(band, n_band - 1, n_band)}]
    greet(places)
    rows, columns, channels = tok.shape
    per_head = rows // n_head
    others = range(1, n_head)
    copies = []
    for off in others:
        to = shift(head, off, n_head)
        c = remote(
            tok.at[pl.ds(to * per_head, per_head)], xs.at[head], send.at[0, off - 1],
            recv.at[0, off - 1], {"head": to},
        )
        c.start()
        copies.append(c)
    up = remote(
        tok.at[pl.ds(rows - margin, margin)], halo.at[0], hsend.at[0], hrecv.at[0],
        {"band": shift(band, 1, n_band)},
    )
    down = remote(
        tok.at[pl.ds(0, margin)], halo.at[1], hsend.at[1], hrecv.at[1],
        {"band": shift(band, n_band - 1, n_band)},
    )

    @pl.when(band < n_band - 1)
    def _():
        up.start()

    @pl.when(band > 0)
    def _():
        down.start()

    for r in range(rows):
        mean, spread = stats_row(tok[r])
        stat[0:1, r * columns : (r + 1) * columns] = mean
        stat[1:2, r * columns : (r + 1) * columns] = spread
    for off in others:
        to = shift(head, off, n_head)
        c = remote(stat, stats.at[head], send.at[1, off - 1], recv.at[1, off - 1], {"head": to})
        c.start()
        copies.append(c)
    xs[head] = tok[pl.ds(head * per_head, per_head)]
    stats[head] = stat[...]
    for c in copies:
        c.wait()

    @pl.when(band < n_band - 1)
    def _():
        up.wait_send()
        down.wait_recv()

    @pl.when(band > 0)
    def _():
        down.wait_send()
        up.wait_recv()


def first_exchange(tokens, n_head, n_band):
    band_rows, columns, channels = tokens.shape
    margin = KER // 2
    outs = [
        jax.ShapeDtypeStruct((n_head, band_rows // n_head, columns, channels), tokens.dtype),
        jax.ShapeDtypeStruct((n_head, 2, band_rows * columns), F32),
        jax.ShapeDtypeStruct((2, margin, columns, channels), tokens.dtype),
    ]
    sem = pltpu.SemaphoreType.DMA
    return pl.pallas_call(
        functools.partial(first_kernel, n_head, n_band, margin),
        out_shape=outs,
        in_specs=[VM],
        out_specs=[VM] * 3,
        scratch_shapes=[pltpu.VMEM((2, band_rows * columns), F32)]
        + [sem((2, n_head - 1))] * 2
        + [sem((2,))] * 2,
        compiler_params=params(collective_id=0, has_side_effects=True),
        name="first_exchange",
    )(tokens)


def prepare_kernel(n_head, n_band, tok, xs, stats, gain, cr, cc, fr, normed, wide, part, edge, comb, turned):
    rows, columns, channels = tok.shape
    head, band = lax.axis_index("head"), lax.axis_index("band")
    mean = stats[0, 0:1]
    for i in range(1, n_head):
        mean = mean + stats[i, 0:1]
    mean = mean * (1.0 / n_head)
    total = jnp.zeros_like(mean)
    for i in range(n_head):
        total = total + stats[i, 1:2] + channels * jnp.square(stats[i, 0:1] - mean)
    inv = lax.rsqrt(total * (1.0 / (n_head * channels)) + EPS)
    comb[...] = jnp.zeros_like(comb)
    comb[0:1, :] = mean
    comb[1:2, :] = inv
    margin = edge.shape[2] // columns
    edge[0] = comb[0:2, (rows - margin) * columns :]
    edge[1] = comb[0:2, : margin * columns]
    for r in range(rows):
        col = comb[:, r * columns : (r + 1) * columns].T
        value = ((tok[r].astype(F32) - col[:, 0:1]) * col[:, 1:2] * gain[head]).astype(BF)
        normed[r] = value
        turned[r * channels : (r + 1) * channels, :] = value.T
    per = xs.shape[1] * columns
    for r in range(xs.shape[1]):
        begin = pl.multiple_of(head * per + r * columns, 128)
        col = comb[:, pl.ds(begin, columns)].T
        for i in range(n_head):
            value = (xs[i, r].astype(F32) - col[:, 0:1]) * col[:, 1:2] * gain[i]
            wide[r * columns : (r + 1) * columns, i * channels : (i + 1) * channels] = value.astype(BF)
    left = (1.0 - fr[1:2]).astype(BF).astype(F32)
    right = fr[1:2].astype(BF).astype(F32)
    top = (1.0 - fr[0:1]).astype(BF).astype(F32)
    bottom = fr[0:1].astype(BF).astype(F32)
    points = cc.shape[1]
    share = channels // n_band
    block = 256

    for begin in range(0, points, block):
        at = slice(begin, begin + block)
        spot = lax.broadcasted_iota(jnp.int32, (columns, block), 0)
        table = jnp.where(
            spot == cc[:, at], left[:, at], jnp.where(spot == cc[:, at] + 1, right[:, at], 0.0)
        ).astype(BF)
        inner = dot(turned[...], table)
        total = jnp.zeros((channels, block), F32)
        for r in range(rows):
            row = band * rows + r
            w = jnp.where(cr[:, at] == row, top[:, at], 0.0) + jnp.where(
                cr[:, at] + 1 == row, bottom[:, at], 0.0
            )
            total = total + w * inner[r * channels : (r + 1) * channels]
        for b in range(n_band):
            part[b, :, at] = total[b * share : (b + 1) * share].astype(BF)


def prepare(tokens, xs, stats, gain, cr, cc, fr, n_head, n_band):
    rows, columns, channels = tokens.shape
    points = cc.shape[1]
    per = xs.shape[1] * columns
    width = n_head * channels
    margin = KER // 2
    return pl.pallas_call(
        functools.partial(prepare_kernel, n_head, n_band),
        out_shape=[
            jax.ShapeDtypeStruct(tokens.shape, BF),
            jax.ShapeDtypeStruct((per, width), BF),
            jax.ShapeDtypeStruct((n_band, channels // n_band, points), BF),
            jax.ShapeDtypeStruct((2, 2, margin * columns), F32),
        ],
        in_specs=[VM] * 7,
        out_specs=[VM] * 4,
        scratch_shapes=[
            pltpu.VMEM((8, rows * columns), F32),
            pltpu.VMEM((rows * channels, columns), BF),
        ],
        compiler_params=params(),
        name="prepare",
    )(tokens, xs, stats, gain, cr, cc, fr)


def second_kernel(
    factor, n_head, n_band,
    part, edge, tok, normed, halo, gain, taps, wide, wq, wk, wv,
    whole, base, query, gk, gv,
    landed, rim, padded, comb, gq, weight,
    bsend, brecv, esend, erecv, zsend, zrecv, hsend, hrecv, wsend, wrecv, dsend, drecv,
):
    head, band, dp = (lax.axis_index(name) for name in ("head", "band", "dp"))
    places = [{"head": shift(head, off, n_head)} for off in range(1, n_head)]
    places += [{"band": shift(band, off, n_band)} for off in range(1, n_band)]
    places += [{"dp": 1 - dp}]
    greet(places)
    bands, heads = range(1, n_band), range(1, n_head)
    up = remote(edge.at[0], rim.at[0], esend.at[0], erecv.at[0], {"band": shift(band, 1, n_band)})
    down = remote(
        edge.at[1], rim.at[1], esend.at[1], erecv.at[1], {"band": shift(band, n_band - 1, n_band)}
    )
    up.start()
    down.start()
    parts = []
    for off in bands:
        to = shift(band, off, n_band)
        c = remote(part.at[to], landed.at[off - 1], bsend.at[off - 1], brecv.at[off - 1], {"band": to})
        c.start()
        parts.append(c)
    pairs = [(wq, gq), (wk, gk), (wv, gv)]
    copies = gather_start(pairs, head, dp, n_head, wsend, wrecv)

    rows, columns, channels = tok.shape
    margin = KER // 2
    side_pad = 8
    padded[:, 0:side_pad, :] = jnp.zeros((rows + 2 * margin, side_pad, channels), F32)
    padded[:, side_pad + columns :, :] = jnp.zeros((rows + 2 * margin, side_pad, channels), F32)
    for r in range(rows):
        padded[margin + r, side_pad : side_pad + columns, :] = normed[r].astype(F32)

    def fill(side):
        comb[...] = jnp.zeros_like(comb)
        comb[0:2, :] = rim[side]
        there = band > 0 if side == 0 else band < n_band - 1
        for r in range(margin):
            col = comb[:, r * columns : (r + 1) * columns].T
            value = (halo[side, r].astype(F32) - col[:, 0:1]) * col[:, 1:2] * gain[head]
            value = jnp.where(there, value.astype(BF).astype(F32), 0.0)
            padded[side * (margin + rows) + r, side_pad : side_pad + columns, :] = value

    block = 64

    def convolve(first, last):
        @pl.loop(first, last)
        def _(r):
            @pl.loop(0, columns // block)
            def _(step):
                begin = pl.multiple_of(step * block, block)
                at = pl.ds(begin, block)
                total = tok[r, at, :].astype(F32)
                for a in range(KER):
                    for b in range(KER):
                        total = total + taps[a * KER + b : a * KER + b + 1, :] * padded[
                            r + a, pl.ds(begin + (side_pad - margin + b), block), :
                        ]
                base[r, at, :] = total

    up.wait()
    down.wait()
    fill(0)
    fill(1)
    convolve(0, rows // 4)

    total = part[band].astype(F32)
    for off in bands:
        parts[off - 1].wait_recv()
        total = total + landed[off - 1].astype(F32)
    whole[band, head] = total.astype(BF)
    along, across = [], []
    for off in bands:
        c = remote(
            whole.at[band, head], whole.at[band, head], zsend.at[off - 1], zrecv.at[off - 1],
            {"band": shift(band, off, n_band)},
        )
        c.start()
        along.append(c)
    for step in range(n_band):
        source = shift(band, n_band - step, n_band)
        if step == 1:
            convolve(rows // 4, rows // 2)
        if step == 2:
            halves = gather_relay(pairs, copies, head, dp, n_head, dsend, drecv)
        if step:
            along[step - 1].wait_recv()
        for off in heads:
            c = remote(
                whole.at[source, head], whole.at[source, head], hsend.at[step, off - 1],
                hrecv.at[step, off - 1], {"head": shift(head, off, n_head)},
            )
            c.start()
            across.append(c)
    convolve(rows // 2, rows)
    gather_finish(copies, halves)
    half = gq.shape[2]
    for a in range(2):
        for i in range(n_head):
            weight[a * half : (a + 1) * half, i * channels : (i + 1) * channels] = gq[a, i]

    @pl.loop(0, wide.shape[0] // 256)
    def _(step):
        at = pl.ds(pl.multiple_of(step * 256, 256), 256)
        query[at, :] = (dot(wide[at, :], weight[...]) * factor).astype(BF)

    for c in across:
        c.wait()
    for c in along + parts:
        c.wait_send()


def second_exchange(part, edge, tokens, normed, halo, gain, taps, wide, wq, wk, wv, n_head, n_band, factor):
    sem = pltpu.SemaphoreType.DMA
    rows, columns, channels = tokens.shape
    margin = KER // 2
    weights = [halved(w) for w in (wq, wk, wv)]
    gathered = [(2, n_head) + w.shape[1:] for w in weights]
    return pl.pallas_call(
        functools.partial(second_kernel, factor, n_head, n_band),
        out_shape=[
            jax.ShapeDtypeStruct((n_band, n_head) + part.shape[1:], BF),
            jax.ShapeDtypeStruct(tokens.shape, F32),
            jax.ShapeDtypeStruct(wide.shape, BF),
            jax.ShapeDtypeStruct(gathered[1], BF),
            jax.ShapeDtypeStruct(gathered[2], BF),
        ],
        in_specs=[VM] * 11,
        out_specs=[VM] * 5,
        scratch_shapes=[
            pltpu.VMEM((n_band - 1,) + part.shape[1:], BF),
            pltpu.VMEM(edge.shape, F32),
            pltpu.VMEM((rows + 2 * margin, columns + 16, channels), F32),
            pltpu.VMEM((8, margin * columns), F32),
            pltpu.VMEM(gathered[0], BF),
            pltpu.VMEM((wide.shape[1], wide.shape[1]), BF),
        ]
        + [sem((n_band - 1,))] * 2
        + [sem((2,))] * 2
        + [sem((n_band - 1,))] * 2
        + [sem((n_band, n_head - 1))] * 2
        + gather_sems(3, n_head),
        compiler_params=params(collective_id=1, has_side_effects=True),
        name="second_exchange",
    )(part, edge, tokens, normed, halo, gain, taps, wide, *weights)


def attend_kernel(
    size, query, samples, gk, gv, wo, base, out,
    sampled, turned, keys, values, go, weight, attended, mine, landed,
    send, recv, wsend, wrecv, dsend, drecv,
):
    n_band, n_head, share, points = samples.shape
    head, dp = lax.axis_index("head"), lax.axis_index("dp")
    greet([{"head": shift(head, off, n_head)} for off in range(1, n_head)] + [{"dp": 1 - dp}])
    pairs = [(wo, go)]
    copies = gather_start(pairs, head, dp, n_head, wsend, wrecv)
    channels = share * n_band
    half = gk.shape[2]
    group = channels // size
    for b in range(n_band):
        for i in range(n_head):
            at = i * channels + b * share
            sampled[at : at + share, :] = samples[b, i]
    turned[...] = sampled[...].T

    @pl.loop(0, n_head)
    def _(i):
        flip = ((0,), (0,))
        key = dot(gk[0, i], sampled[0:half, :], flip) + dot(gk[1, i], sampled[half:, :], flip)
        value = dot(turned[:, 0:half], gv[0, i]) + dot(turned[:, half:], gv[1, i])
        key_spot = lax.broadcasted_iota(jnp.int32, key.shape, 0)
        value_spot = lax.broadcasted_iota(jnp.int32, value.shape, 1)
        for j in range(group):
            low_end, high_end = j * size, (j + 1) * size
            keep = (key_spot >= low_end) & (key_spot < high_end)
            keys[i * group + j] = jnp.where(keep, key, 0.0).astype(BF)
            keep = (value_spot >= low_end) & (value_spot < high_end)
            values[i * group + j, :, 0:channels] = jnp.where(keep, value, 0.0).astype(BF)
            values[i * group + j, :, channels:] = jnp.ones((points, channels), BF)

    halves = gather_relay(pairs, copies, head, dp, n_head, dsend, drecv)
    gather_finish(copies, halves)
    low = go.shape[2]
    for a in range(2):
        for i in range(n_head):
            at = i * channels + a * low
            weight[at : at + low, :] = go[a, i]
    block = attended.shape[0]
    steps = query.shape[0] // block

    def back(step, off):
        at = pl.ds(pl.multiple_of(step * block, block), block)
        to = shift(head, off, n_head)
        return remote(
            mine.at[to, at], landed.at[head, at], send.at[step, off - 1], recv.at[step, off - 1],
            {"head": to},
        )

    @pl.loop(0, steps)
    def _(step):
        at = pl.ds(pl.multiple_of(step * block, block), block)

        def score(h):
            i = h // group
            return dot(query[at, i * channels : (i + 1) * channels], keys[h])

        following = score(0)
        for i in range(n_head):
            total = jnp.zeros((block, channels), F32)
            for j in range(group):
                h = i * group + j
                current = following
                if h + 1 < n_head * group:
                    following = score(h + 1)
                top = jnp.max(current, axis=1, keepdims=True)
                prob = jnp.exp2(current - top).astype(BF)
                both = dot(prob, values[h])
                total = total + both[:, 0:channels] / both[:, channels:]
            attended[:, i * channels : (i + 1) * channels] = total.astype(BF)
        result = dot(attended[...], weight[...])
        for i in range(n_head):
            mine[i, at, :] = result[:, i * channels : (i + 1) * channels].astype(BF)
        for off in range(1, n_head):
            back(step, off).start()

    out[head] = (base[head] + mine[head].astype(F32)).astype(BF)
    for off in range(1, n_head):
        source = shift(head, n_head - off, n_head)
        for step in range(steps):
            back(step, off).wait()
        out[source] = (base[source] + landed[source].astype(F32)).astype(BF)


def attend(query, samples, gk, gv, wo, base):
    n_band, n_head, share, points = samples.shape
    count, width = query.shape
    channels = width // n_head
    block = 256
    wo = halved(wo)
    base = base.reshape(n_head, count, channels)
    return pl.pallas_call(
        functools.partial(attend_kernel, width // HEADS),
        out_shape=jax.ShapeDtypeStruct((n_head, count, channels), BF),
        in_specs=[VM] * 6,
        out_specs=VM,
        scratch_shapes=[
            pltpu.VMEM((width, points), BF),
            pltpu.VMEM((points, width), BF),
            pltpu.VMEM((HEADS, channels, points), BF),
            pltpu.VMEM((HEADS, points, 2 * channels), BF),
            pltpu.VMEM((2, n_head) + wo.shape[1:], BF),
            pltpu.VMEM((width, width), BF),
            pltpu.VMEM((block, width), BF),
            pltpu.VMEM((n_head, count, channels), BF),
            pltpu.VMEM((n_head, count, channels), BF),
        ]
        + [pltpu.SemaphoreType.DMA((count // block, n_head - 1))] * 2
        + gather_sems(1, n_head),
        compiler_params=params(collective_id=2, has_side_effects=True),
        name="attend",
    )(query, samples, gk, gv, wo, base)


def shards(
    tokens, corner_row, corner_col, fraction, w_query, w_key, w_value, w_out, conv_kernel, norm_gain
):
    n_head, n_band = lax.axis_size("head"), lax.axis_size("band")
    channels = tokens.shape[2]
    width = n_head * channels
    factor = math.log2(math.e) / math.sqrt(width // HEADS)
    gain = norm_gain.reshape(n_head, 1, channels)
    xs, stats, halo = first_exchange(tokens, n_head, n_band)
    normed, wide, part, edge = prepare(
        tokens, xs, stats, gain, corner_row[None], corner_col[None], fraction, n_head, n_band
    )
    samples, base, query, gk, gv = second_exchange(
        part, edge, tokens, normed, halo, gain, conv_kernel, wide, w_query, w_key, w_value,
        n_head, n_band, factor,
    )
    return attend(query, samples, gk, gv, w_out, base).reshape(tokens.shape)


def solution(mesh):
    return jax.shard_map(
        shards,
        mesh=mesh,
        in_specs=(
            P(("dp", "band"), None, "head"),
            P("dp"),
            P("dp"),
            P(None, "dp"),
            P(None, "head"),
            P(None, "head"),
            P(None, "head"),
            P("head", None),
            P(None, "head"),
            P(),
        ),
        out_specs=P(("dp", "band"), None, "head"),
        check_vma=False,
    )
```

time: 135 us -> 96 us (0.71)
  Pallas kernels: 134 us -> 93.5 us
  local copies, waits for them, and re-layouts: 0 us -> 2.26 us
    pallas_call x5 -> x2, Pallas kernels: 60.4 us -> 33.9 us  [the longest x1 27.8 us: second_exchange(): pl.pallas_call(functools.partial(second_kernel, factor, n_head, n_band),...]
    pallas_call x1, Pallas kernels: 36.1 us -> 23 us  [first_exchange(): pl.pallas_call(functools.partial(first_kernel, n_head, n_band, margin), o...]
    unnamed x0 -> x1, local copies, waits for them, and re-layouts: none -> 2.26 us
where the time goes in v2:
time: 96 us; the launch traced here: 95.8 us
  Pallas kernels  93.5 us (97%)
  local copies, waits for them, and re-layouts  2.26 us (2%)
    pallas_call x1, Pallas kernels, attend(): pl.pallas_call(functools.partial(attend_kernel, width // HEADS), out_shap...  36.6 us
    pallas_call x1, Pallas kernels, second_exchange(): pl.pallas_call(functools.partial(second_kernel, factor, n_head, n_band),...  27.8 us
    pallas_call x1, Pallas kernels, first_exchange(): pl.pallas_call(functools.partial(first_kernel, n_head, n_band, margin), o...  23 us
    pallas_call x1, Pallas kernels, prepare(): pl.pallas_call(functools.partial(prepare_kernel, n_head, n_band), out_sha...  6.09 us
    unnamed x1, local copies, waits for them, and re-layouts  2.26 us

profile of v2, /device:TPU:0, one launch (start us, length us, event | category | flops | bytes accessed | tf_op | source)
XLA Modules:
  0.0 95.8 jit_solution(8078218316475440599)
XLA Ops:
  0.0 23.0 %first_exchange.1 = (bf16[4,1,1024,128]{3,2,1,0:T(8,128)(2,1)}, f32[4,2,4096]{2,1,0:T(2,128)}, bf16[2,2,1024,128]{3,2,1,0:T(8,128)(2,1)}) custom-call(bf16[4,1024,128]{2,1,0:T(8,128)(2,1)} %tok.5), custom_call_target="tpu_custom_call" | custom-call | tf_op jit(solution)/shard_map/first_exchange/pallas_call | solution.py:172
  23.0 6.1 %prepare.1 = (bf16[4,1024,128]{2,1,0:T(8,128)(2,1)}, bf16[1024,512]{1,0:T(8,128)(2,1)}, bf16[4,32,1024]{2,1,0:T(8,128)(2,1)}, f32[2,2,2048]{2,1,0:T(2,128)}) custom-call(bf16[4,1024,128]{2,1,0:T(8,128)(2,1)} %tok.5, bf16[4,1,1024,128]{3,2,1,0:T(8,128)(2,1)} %get-tuple-element.17.xs, f32[4,2,4096]{2,1,0:T(2,128)} %get-tuple-element.18.stats, ...), custom_call_target="tpu_custom_call" | custom-call | tf_op jit(solution)/shard_map/prepare/pallas_call | solution.py:246
  29.1 27.8 %second_exchange.1 = (bf16[4,4,32,1024]{3,2,1,0:T(8,128)(2,1)}, f32[4,1024,128]{2,1,0:T(8,128)}, bf16[1024,512]{1,0:T(8,128)(2,1)}, bf16[2,4,256,128]{3,2,1,0:T(8,128)(2,1)}, bf16[2,4,256,128]{3,2,1,0:T(8,128)(2,1)}) custom-call(bf16[4,32,1024]{2,1,0:T(8,128)(2,1)} %get-tuple-element.19.part, f32[2,2,2048]{2,1,0:T(2,128)} %get-tuple-element.20.edge, ...), custom_call_target="tpu_custom_call" | custom-call | tf_op jit(solution)/shard_map/second_exchange/pallas_call | solution.py:386
  56.9 36.6 %attend.1 = bf16[4,1024,128]{2,1,0:T(8,128)(2,1)} custom-call(bf16[1024,512]{1,0:T(8,128)(2,1)} %get-tuple-element.24.query, bf16[4,4,32,1024]{3,2,1,0:T(8,128)(2,1)} %get-tuple-element.25.samples, bf16[2,4,256,128]{3,2,1,0:T(8,128)(2,1)} %get-tuple-element.26.gk, bf16[2,4,256,128]{3,2,1,0:T(8,128)(2,1)} %get-tuple-element.27.gv, ...), custom_call_target="tpu_custom_call" | custom-call | tf_op jit(solution)/shard_map/attend/pallas_call | solution.py:509
  93.5 2.3 %copy.12 = bf16[4,1024,128]{2,1,0:T(8,128)(2,1)} copy(bf16[4,1024,128]{2,1,0:T(8,128)(2,1)} %attend.1) | data formatting | bytes 2097152

commit v3 on v0

v3 whole, which is shorter than its diff:
```python
import functools
import math

import jax
import jax.numpy as jnp
from jax import lax
from jax.experimental import pallas as pl
from jax.experimental.pallas import tpu as pltpu
from jax.sharding import PartitionSpec as P

HEADS = 16
KER = 5
EPS = 1e-05
BF = jnp.bfloat16
F32 = jnp.float32
VM = pl.BlockSpec(memory_space=pltpu.VMEM)


def params(**more):
    return pltpu.CompilerParams(vmem_limit_bytes=44 * 1024 * 1024, **more)


def dot(a, b, dims=((1,), (0,))):
    return lax.dot_general(a, b, (dims, ((), ())), preferred_element_type=F32)


def shift(me, off, count):
    return lax.rem(me + off, count)


def remote(src, dst, send, recv, where):
    return pltpu.make_async_remote_copy(
        src_ref=src,
        dst_ref=dst,
        send_sem=send,
        recv_sem=recv,
        device_id=where,
        device_id_type=pl.DeviceIdType.MESH,
    )


def greet(places):
    barrier = pltpu.get_barrier_semaphore()
    for where in places:
        pl.semaphore_signal(barrier, inc=1, device_id=where, device_id_type=pl.DeviceIdType.MESH)
    pl.semaphore_wait(barrier, len(places))


def gather_start(pairs, head, dp, n_head, sems):
    copies = {}
    for off in range(1, n_head):
        to = shift(head, off, n_head)
        for k, src, dst in pairs:
            c = remote(src.at[dp], dst.at[dp, head], sems[0].at[k, off - 1], sems[1].at[k, off - 1], {"head": to})
            c.start()
            copies[k, off] = c
    for k, src, dst in pairs:
        dst[dp, head] = src[dp]
        dst[1 - dp, head] = src[1 - dp]
    return copies


def gather_relay(pairs, copies, head, dp, n_head, sems):
    halves = []
    for off in range(1, n_head):
        back = shift(head, n_head - off, n_head)
        for k, src, dst in pairs:
            copies[k, off].wait_recv()
            c = remote(
                dst.at[dp, back], dst.at[dp, back], sems[2].at[k, off - 1], sems[3].at[k, off - 1],
                {"dp": 1 - dp},
            )
            c.start()
            halves.append(c)
    return halves


def gather_finish(copies, halves):
    for c in copies.values():
        c.wait_send()
    for c in halves:
        c.wait()


def halved(w):
    return w.reshape(2, w.shape[0] // 2, w.shape[1])


def stats_row(x):
    channels = x.shape[1]
    part = 1.0 / channels
    mean = dot(x, jnp.full((channels, channels), part, BF))
    square = jnp.square(x.astype(F32) - mean)
    high = square.astype(BF)
    low = (square - high.astype(F32)).astype(BF)
    ones = jnp.ones((8, channels), BF)
    rows = ((1,), (1,))
    mean_row = dot(jnp.full((8, channels), part, BF), x, rows)
    spread_row = dot(ones, high, rows) + dot(ones, low, rows)
    return mean_row[0:1], spread_row[0:1]


def block_kernel(
    size, factor, n_head, n_band,
    tok, gain, cr, cc, fr, taps, wq, wk, wv, wo,
    base, landed,
    xs, stat, stats, comb, halo, rim, edge, padded, side_comb, turned, table, part, arrived, whole,
    wide, query, gq, gk, gv, go, weight, sampled, flipped, keys, values, attended, mine,
    ssend, srecv, tsend, trecv, lsend, lrecv, esend, erecv, bsend, brecv, zsend, zrecv,
    asend, arecv, wsend, wrecv, dsend, drecv, osend, orecv,
):
    head, band, dp = (lax.axis_index(name) for name in ("head", "band", "dp"))
    bands, heads = range(1, n_band), range(1, n_head)
    places = [{"head": shift(head, off, n_head)} for off in heads]
    places += [{"band": shift(band, off, n_band)} for off in bands]
    places += [{"dp": 1 - dp}]
    rows, columns, channels = tok.shape
    margin = KER // 2
    per_head = rows // n_head
    side_pad = 8
    greet(places)

    sems = (wsend, wrecv, dsend, drecv)
    early = [(0, wq, gq)]
    later = [(1, wk, gk), (2, wv, gv)]
    last = [(3, wo, go)]
    copies = gather_start(early, head, dp, n_head, sems)
    after = {"band": shift(band, 1, n_band)}
    before = {"band": shift(band, n_band - 1, n_band)}
    up = remote(tok.at[pl.ds(rows - margin, margin)], halo.at[0], lsend.at[0], lrecv.at[0], after)
    down = remote(tok.at[pl.ds(0, margin)], halo.at[1], lsend.at[1], lrecv.at[1], before)

    @pl.when(band < n_band - 1)
    def _():
        up.start()

    @pl.when(band > 0)
    def _():
        down.start()

    for r in range(rows):
        mean, spread = stats_row(tok[r])
        stat[0:1, r * columns : (r + 1) * columns] = mean
        stat[1:2, r * columns : (r + 1) * columns] = spread
    told, moved = [], []
    for off in heads:
        c = remote(
            stat, stats.at[head], ssend.at[off - 1], srecv.at[off - 1],
            {"head": shift(head, off, n_head)},
        )
        c.start()
        told.append(c)
    for off in heads:
        to = shift(head, off, n_head)
        c = remote(
            tok.at[pl.ds(to * per_head, per_head)], xs.at[head], tsend.at[off - 1],
            trecv.at[off - 1], {"head": to},
        )
        c.start()
        moved.append(c)
    copies.update(gather_start(later, head, dp, n_head, sems))
    stats[head] = stat[...]
    xs[head] = tok[pl.ds(head * per_head, per_head)]

    left = (1.0 - fr[1:2]).astype(BF).astype(F32)
    right = fr[1:2].astype(BF).astype(F32)
    top = (1.0 - fr[0:1]).astype(BF).astype(F32)
    bottom = fr[0:1].astype(BF).astype(F32)
    points = cc.shape[1]
    share = channels // n_band
    chunk = 256
    for begin in range(0, points, chunk):
        at = slice(begin, begin + chunk)
        spot = lax.broadcasted_iota(jnp.int32, (columns, chunk), 0)
        table[:, at] = jnp.where(
            spot == cc[:, at], left[:, at], jnp.where(spot == cc[:, at] + 1, right[:, at], 0.0)
        ).astype(BF)
    padded[:, 0:side_pad, :] = jnp.zeros((rows + 2 * margin, side_pad, channels), F32)
    padded[:, side_pad + columns :, :] = jnp.zeros((rows + 2 * margin, side_pad, channels), F32)
    comb[...] = jnp.zeros_like(comb)
    side_comb[...] = jnp.zeros_like(side_comb)

    for c in told:
        c.wait()
    mean = stats[0, 0:1]
    for i in range(1, n_head):
        mean = mean + stats[i, 0:1]
    mean = mean * (1.0 / n_head)
    total = jnp.zeros_like(mean)
    for i in range(n_head):
        total = total + stats[i, 1:2] + channels * jnp.square(stats[i, 0:1] - mean)
    comb[0:1, :] = mean
    comb[1:2, :] = lax.rsqrt(total * (1.0 / (n_head * channels)) + EPS)
    edge[0] = comb[0:2, (rows - margin) * columns :]
    edge[1] = comb[0:2, : margin * columns]
    rim_up = remote(edge.at[0], rim.at[0], esend.at[0], erecv.at[0], after)
    rim_down = remote(edge.at[1], rim.at[1], esend.at[1], erecv.at[1], before)
    rim_up.start()
    rim_down.start()
    for r in range(rows):
        col = comb[:, r * columns : (r + 1) * columns].T
        value = ((tok[r].astype(F32) - col[:, 0:1]) * col[:, 1:2] * gain[head]).astype(BF)
        padded[margin + r, side_pad : side_pad + columns, :] = value.astype(F32)
        turned[r * channels : (r + 1) * channels, :] = value.T
    for begin in range(0, points, chunk):
        at = slice(begin, begin + chunk)
        inner = dot(turned[...], table[:, at])
        total = jnp.zeros((channels, chunk), F32)
        for r in range(rows):
            row = band * rows + r
            w = jnp.where(cr[:, at] == row, top[:, at], 0.0) + jnp.where(
                cr[:, at] + 1 == row, bottom[:, at], 0.0
            )
            total = total + w * inner[r * channels : (r + 1) * channels]
        for b in range(n_band):
            part[b, :, at] = total[b * share : (b + 1) * share].astype(BF)
    parts = []
    for off in bands:
        to = shift(band, off, n_band)
        c = remote(part.at[to], arrived.at[off - 1], bsend.at[off - 1], brecv.at[off - 1], {"band": to})
        c.start()
        parts.append(c)

    def fill(side):
        side_comb[0:2, :] = rim[side]
        there = band > 0 if side == 0 else band < n_band - 1
        for r in range(margin):
            col = side_comb[:, r * columns : (r + 1) * columns].T
            value = (halo[side, r].astype(F32) - col[:, 0:1]) * col[:, 1:2] * gain[head]
            value = jnp.where(there, value.astype(BF).astype(F32), 0.0)
            padded[side * (margin + rows) + r, side_pad : side_pad + columns, :] = value

    tile = 64

    def convolve(first, end):
        @pl.loop(first, end)
        def _(r):
            @pl.loop(0, columns // tile)
            def _(step):
                begin = pl.multiple_of(step * tile, tile)
                at = pl.ds(begin, tile)
                total = tok[r, at, :].astype(F32)
                for a in range(KER):
                    for b in range(KER):
                        total = total + taps[a * KER + b : a * KER + b + 1, :] * padded[
                            r + a, pl.ds(begin + (side_pad - margin + b), tile), :
                        ]
                base[r, at, :] = total

    rim_up.wait()
    rim_down.wait()

    @pl.when(band < n_band - 1)
    def _():
        up.wait_send()
        down.wait_recv()

    @pl.when(band > 0)
    def _():
        down.wait_send()
        up.wait_recv()

    fill(0)
    fill(1)
    convolve(0, rows // 4)

    total = part[band].astype(F32)
    for off in bands:
        parts[off - 1].wait_recv()
        total = total + arrived[off - 1].astype(F32)
    whole[band, head] = total.astype(BF)
    along, across = [], []
    for off in bands:
        c = remote(
            whole.at[band, head], whole.at[band, head], zsend.at[off - 1], zrecv.at[off - 1],
            {"band": shift(band, off, n_band)},
        )
        c.start()
        along.append(c)
    for step in range(n_band):
        source = shift(band, n_band - step, n_band)
        if step == 1:
            convolve(rows // 4, rows // 2)
        if step:
            along[step - 1].wait_recv()
        for off in heads:
            c = remote(
                whole.at[source, head], whole.at[source, head], asend.at[step, off - 1],
                arecv.at[step, off - 1], {"head": shift(head, off, n_head)},
            )
            c.start()
            across.append(c)
    copies.update(gather_start(last, head, dp, n_head, sems))
    halves = gather_relay(early + later, copies, head, dp, n_head, sems)
    convolve(rows // 2, rows)

    for c in moved:
        c.wait()
    per = per_head * columns
    for r in range(per_head):
        begin = pl.multiple_of(head * per + r * columns, 128)
        col = comb[:, pl.ds(begin, columns)].T
        for i in range(n_head):
            value = (xs[i, r].astype(F32) - col[:, 0:1]) * col[:, 1:2] * gain[i]
            wide[r * columns : (r + 1) * columns, i * channels : (i + 1) * channels] = value.astype(BF)
    for c in halves:
        c.wait()
    half = gq.shape[2]
    for a in range(2):
        for i in range(n_head):
            weight[a * half : (a + 1) * half, i * channels : (i + 1) * channels] = gq[a, i]

    @pl.loop(0, per // 256)
    def _(step):
        at = pl.ds(pl.multiple_of(step * 256, 256), 256)
        query[at, :] = (dot(wide[at, :], weight[...]) * factor).astype(BF)

    for c in across:
        c.wait()
    for c in along + parts:
        c.wait_send()

    group = channels // size
    for b in range(n_band):
        for i in range(n_head):
            at = i * channels + b * share
            sampled[at : at + share, :] = whole[b, i]
    flipped[...] = sampled[...].T

    @pl.loop(0, n_head)
    def _(i):
        flip = ((0,), (0,))
        key = dot(gk[0, i], sampled[0:half, :], flip) + dot(gk[1, i], sampled[half:, :], flip)
        value = dot(flipped[:, 0:half], gv[0, i]) + dot(flipped[:, half:], gv[1, i])
        key_spot = lax.broadcasted_iota(jnp.int32, key.shape, 0)
        value_spot = lax.broadcasted_iota(jnp.int32, value.shape, 1)
        for j in range(group):
            low_end, high_end = j * size, (j + 1) * size
            keep = (key_spot >= low_end) & (key_spot < high_end)
            keys[i * group + j] = jnp.where(keep, key, 0.0).astype(BF)
            keep = (value_spot >= low_end) & (value_spot < high_end)
            values[i * group + j, :, 0:channels] = jnp.where(keep, value, 0.0).astype(BF)
            values[i * group + j, :, channels:] = jnp.ones((points, channels), BF)

    halves = gather_relay(last, copies, head, dp, n_head, sems)
    gather_finish(copies, halves)
    low = go.shape[2]
    for a in range(2):
        for i in range(n_head):
            at = i * channels + a * low
            weight[at : at + low, :] = go[a, i]
    block = attended.shape[0]
    steps = query.shape[0] // block

    def back(step, off):
        at = pl.ds(pl.multiple_of(step * block, block), block)
        to = shift(head, off, n_head)
        return remote(
            mine.at[to, at], landed.at[head, at], osend.at[step, off - 1], orecv.at[step, off - 1],
            {"head": to},
        )

    @pl.loop(0, steps)
    def _(step):
        at = pl.ds(pl.multiple_of(step * block, block), block)

        def score(h):
            i = h // group
            return dot(query[at, i * channels : (i + 1) * channels], keys[h])

        following = score(0)
        for i in range(n_head):
            total = jnp.zeros((block, channels), F32)
            for j in range(group):
                h = i * group + j
                current = following
                if h + 1 < n_head * group:
                    following = score(h + 1)
                top = jnp.max(current, axis=1, keepdims=True)
                prob = jnp.exp2(current - top).astype(BF)
                both = dot(prob, values[h])
                total = total + both[:, 0:channels] / both[:, channels:]
            attended[:, i * channels : (i + 1) * channels] = total.astype(BF)
        result = dot(attended[...], weight[...])
        for i in range(n_head):
            mine[i, at, :] = result[:, i * channels : (i + 1) * channels].astype(BF)
        for off in heads:
            back(step, off).start()

    landed[head] = mine[head]
    for off in heads:
        for step in range(steps):
            back(step, off).wait()


def run_block(tokens, gain, cr, cc, fr, taps, wq, wk, wv, wo, n_head, n_band):
    rows, columns, channels = tokens.shape
    width = n_head * channels
    size = width // HEADS
    points = cc.shape[1]
    share = channels // n_band
    margin = KER // 2
    per_head = rows // n_head
    count = per_head * columns
    block = 256
    weights = [halved(w) for w in (wq, wk, wv, wo)]
    factor = math.log2(math.e) / math.sqrt(size)
    V = pltpu.VMEM
    sem = pltpu.SemaphoreType.DMA
    scratch = [
        V((n_head, per_head, columns, channels), BF),
        V((2, rows * columns), F32),
        V((n_head, 2, rows * columns), F32),
        V((8, rows * columns), F32),
        V((2, margin, columns, channels), BF),
        V((2, 2, margin * columns), F32),
        V((2, 2, margin * columns), F32),
        V((rows + 2 * margin, columns + 16, channels), F32),
        V((8, margin * columns), F32),
        V((rows * channels, columns), BF),
        V((columns, points), BF),
        V((n_band, share, points), BF),
        V((n_band - 1, share, points), BF),
        V((n_band, n_head, share, points), BF),
        V((count, width), BF),
        V((count, width), BF),
    ]
    scratch += [V((2, n_head) + w.shape[1:], BF) for w in weights]
    scratch += [
        V((width, width), BF),
        V((width, points), BF),
        V((points, width), BF),
        V((HEADS, channels, points), BF),
        V((HEADS, points, 2 * channels), BF),
        V((block, width), BF),
        V((n_head, count, channels), BF),
    ]
    for shape in (
        (n_head - 1,), (n_head - 1,), (2,), (2,), (n_band - 1,), (n_band - 1,),
        (n_band, n_head - 1), (4, n_head - 1), (4, n_head - 1), (count // block, n_head - 1),
    ):
        scratch += [sem(shape)] * 2
    return pl.pallas_call(
        functools.partial(block_kernel, size, factor, n_head, n_band),
        out_shape=[
            jax.ShapeDtypeStruct(tokens.shape, F32),
            jax.ShapeDtypeStruct((n_head, count, channels), BF),
        ],
        in_specs=[VM] * 10,
        out_specs=[VM] * 2,
        scratch_shapes=scratch,
        compiler_params=params(collective_id=0, has_side_effects=True),
        name="block",
    )(tokens, gain, cr, cc, fr, taps, *weights)


def shards(
    tokens, corner_row, corner_col, fraction, w_query, w_key, w_value, w_out, conv_kernel, norm_gain
):
    n_head, n_band = lax.axis_size("head"), lax.axis_size("band")
    channels = tokens.shape[2]
    base, projected = run_block(
        tokens, norm_gain.reshape(n_head, 1, channels), corner_row[None], corner_col[None], fraction,
        conv_kernel, w_query, w_key, w_value, w_out, n_head, n_band,
    )
    return (base + projected.reshape(tokens.shape).astype(F32)).astype(BF)


def solution(mesh):
    return jax.shard_map(
        shards,
        mesh=mesh,
        in_specs=(
            P(("dp", "band"), None, "head"),
            P("dp"),
            P("dp"),
            P(None, "dp"),
            P(None, "head"),
            P(None, "head"),
            P(None, "head"),
            P("head", None),
            P(None, "head"),
            P(),
        ),
        out_specs=P(("dp", "band"), None, "head"),
        check_vma=False,
    )
```

time: 303 us -> 82.1 us (0.27)
  waiting for transfers between devices: 113 us -> 0 us
  Pallas kernels: 0 us -> 72.2 us
  matrix products: 63.1 us -> 0 us
  other arithmetic: 42 us -> 1.18 us
  blocking collectives: 37.5 us -> 0 us
  local copies, waits for them, and re-layouts: 29.8 us -> 8.31 us
  between operations: 13.4 us -> 0.02 us
    pallas_call x0 -> x1, Pallas kernels: none -> 72.2 us  [run_block(): pl.pallas_call(functools.partial(block_kernel, size, factor, n_head, n_ba...]
    all_gather x1 -> x0, waiting for transfers between devices: 53.4 us -> none  [shards(): whole = lax.all_gather(tokens, 'head', axis=2, tiled=True)]
    dot_general x16 -> x0, matrix products: 39.7 us -> none  [the longest x8 24.7 us: one_block(): jnp.einsum('hqk,khd->qhd', probs, value_heads, preferred_element_type=jnp...]
    all_gather x3 -> x0, blocking collectives: 37.5 us -> none  [the longest x1 14.3 us: shards(): lax.all_gather(key_share, 'band', axis=0, tiled=True)]
    unnamed x4 -> x0, waiting for transfers between devices: 34.9 us -> none
    convert_element_type x6 -> x1, other arithmetic: 35.3 us -> 1.18 us  [shards(): return (base + projected.reshape(tokens.shape).astype(F32)).astype(BF)]
    sub x8 -> x0, matrix products: 23.4 us -> none  [one_block(): expo = jnp.exp(scores - top)]
    reduce_scatter x1 -> x0, waiting for transfers between devices: 15.3 us -> none  [shards(): lax.psum_scatter(sample_points(normed_here, col_table, row_table, share_r...]
  transfers between devices with their start and end apart: 5 -> 0, of which waited for: 5 -> 0; matrix products, arithmetic and copies ran while one was open for 4% -> 0% of each run, Pallas kernels for 0% -> 0%
where the time goes in v3:
time: 82.1 us; the launch traced here: 81.7 us
  Pallas kernels  72.2 us (88%)
  local copies, waits for them, and re-layouts  8.31 us (10%)
  other arithmetic  1.18 us (1%)
    pallas_call x1, Pallas kernels, run_block(): pl.pallas_call(functools.partial(block_kernel, size, factor, n_head, n_ba...  72.2 us
    unnamed x20, local copies, waits for them, and re-layouts  8.31 us

profile of v3, /device:TPU:0, one launch (start us, length us, event | category | flops | bytes accessed | tf_op | source)
XLA Modules:
  0.0 81.7 jit_solution(9661279447061682449)
XLA Ops:
  0.0 0.0 copy-start
  0.0 1.2 %copy-done = bf16[4,1024,128]{2,1,0:T(8,128)(2,1)S(1)} copy-done((bf16[4,1024,128]{2,1,0:T(8,128)(2,1)S(1)}, bf16[4,1024,128]{2,1,0:T(8,128)(2,1)}, u32[]{:S(2)}) %copy-start) | copy-done | bytes 1048600
  1.2 0.0 copy-start.1
  1.2 0.9 %copy-done.1 = bf16[512,128]{1,0:T(8,128)(2,1)S(1)} copy-done((bf16[512,128]{1,0:T(8,128)(2,1)S(1)}, bf16[512,128]{1,0:T(8,128)(2,1)}, u32[]{:S(2)}) %copy-start.1) | copy-done | bytes 131096
  2.1 0.0 copy-start.2
  2.1 0.9 %copy-done.2 = bf16[512,128]{1,0:T(8,128)(2,1)S(1)} copy-done((bf16[512,128]{1,0:T(8,128)(2,1)S(1)}, bf16[512,128]{1,0:T(8,128)(2,1)}, u32[]{:S(2)}) %copy-start.2) | copy-done | bytes 131096
  3.0 0.0 copy-start.3
  3.0 0.9 %copy-done.3 = bf16[512,128]{1,0:T(8,128)(2,1)S(1)} copy-done((bf16[512,128]{1,0:T(8,128)(2,1)S(1)}, bf16[512,128]{1,0:T(8,128)(2,1)}, u32[]{:S(2)}) %copy-start.3) | copy-done | bytes 131096
  3.9 0.0 copy-start.4
  3.9 0.9 %copy-done.4 = bf16[128,512]{1,0:T(8,128)(2,1)S(1)} copy-done((bf16[128,512]{1,0:T(8,128)(2,1)S(1)}, bf16[128,512]{1,0:T(8,128)(2,1)}, u32[]{:S(2)}) %copy-start.4) | copy-done | bytes 131096
  4.8 0.0 copy-start.5
  4.8 0.7 copy-done.5
  5.6 0.0 copy-start.6
  5.6 0.7 copy-done.6
  6.3 0.0 copy-start.7
  6.3 0.7 copy-done.7
  6.9 0.0 copy-start.8
  6.9 0.7 copy-done.8
  7.6 0.0 copy-start.9
  7.6 0.7 copy-done.9
  8.3 72.2 %block.1 = (f32[4,1024,128]{2,1,0:T(8,128)S(1)}, bf16[4,1024,128]{2,1,0:T(8,128)(2,1)S(1)}) custom-call(bf16[4,1024,128]{2,1,0:T(8,128)(2,1)S(1)} %copy-done, f32[4,1,128]{2,1,0:T(1,128)S(1)} %bitcast.13, s32[1,1024]{1,0:T(1,128)S(1)} %bitcast.11, s32[1,1024]{1,0:T(1,128)S(1)} %bitcast.12, f32[2,1024]{1,0:T(2,128)S(1)} %copy-done.6, ...), custom_call_target="tpu_custom_call" | custom-call | tf_op jit(solution)/shard_map/block/pallas_call | solution.py:443
  80.5 1.2 %add_convert_fusion = bf16[4,1024,128]{2,1,0:T(8,128)(2,1)} fusion(f32[4,1024,128]{2,1,0:T(8,128)S(1)} %get-tuple-element.7, bf16[4,1024,128]{2,1,0:T(8,128)(2,1)S(1)} %get-tuple-element.8), kind=kLoop, calls=%fused_computation | loop fusion | flops 1572864 | bytes 4194304 | tf_op jit(solution)/shard_map/convert_element_type | solution.py:466
Async XLA Ops:
  0.0 1.2 %copy-start = (bf16[4,1024,128]{2,1,0:T(8,128)(2,1)S(1)}, bf16[4,1024,128]{2,1,0:T(8,128)(2,1)}, u32[]{:S(2)}) copy-start(bf16[4,1024,128]{2,1,0:T(8,128)(2,1)} %tok.1) | copy-start | bytes 3145732
  1.2 0.9 %copy-start.1 = (bf16[512,128]{1,0:T(8,128)(2,1)S(1)}, bf16[512,128]{1,0:T(8,128)(2,1)}, u32[]{:S(2)}) copy-start(bf16[512,128]{1,0:T(8,128)(2,1)} %param.14) | copy-start | bytes 393220
  2.1 0.9 %copy-start.2 = (bf16[512,128]{1,0:T(8,128)(2,1)S(1)}, bf16[512,128]{1,0:T(8,128)(2,1)}, u32[]{:S(2)}) copy-start(bf16[512,128]{1,0:T(8,128)(2,1)} %param.15) | copy-start | bytes 393220
  3.0 0.9 %copy-start.3 = (bf16[512,128]{1,0:T(8,128)(2,1)S(1)}, bf16[512,128]{1,0:T(8,128)(2,1)}, u32[]{:S(2)}) copy-start(bf16[512,128]{1,0:T(8,128)(2,1)} %param.16) | copy-start | bytes 393220
  3.9 0.9 %copy-start.4 = (bf16[128,512]{1,0:T(8,128)(2,1)S(1)}, bf16[128,512]{1,0:T(8,128)(2,1)}, u32[]{:S(2)}) copy-start(bf16[128,512]{1,0:T(8,128)(2,1)} %param.17) | copy-start | bytes 393220
  4.8 0.7 copy-start.5
  5.6 0.7 copy-start.6
  6.3 0.7 copy-start.7
  6.9 0.7 copy-start.8
  7.6 0.7 copy-start.9

commit v4 on v3

--- a/solution.py
+++ b/solution.py
@@ -17,7 +17,7 @@
 
 
 def params(**more):
-    return pltpu.CompilerParams(vmem_limit_bytes=44 * 1024 * 1024, **more)
+    return pltpu.CompilerParams(vmem_limit_bytes=60 * 1024 * 1024, **more)
 
 
 def dot(a, b, dims=((1,), (0,))):
@@ -54,9 +54,6 @@
             c = remote(src.at[dp], dst.at[dp, head], sems[0].at[k, off - 1], sems[1].at[k, off - 1], {"head": to})
             c.start()
             copies[k, off] = c
-    for k, src, dst in pairs:
-        dst[dp, head] = src[dp]
-        dst[1 - dp, head] = src[1 - dp]
     return copies
 
 
@@ -102,12 +99,12 @@
 
 def block_kernel(
     size, factor, n_head, n_band,
-    tok, gain, cr, cc, fr, taps, wq, wk, wv, wo,
-    base, landed,
-    xs, stat, stats, comb, halo, rim, edge, padded, side_comb, turned, table, part, arrived, whole,
+    tok_in, gain_in, cr_in, cc_in, fr_in, taps_in, wq, wk, wv, wo,
+    base_out, landed,
+    tok, gain, cr, cc, fr, taps, base, xs, stat, stats, comb, halo, rim, edge, padded, side_comb, turned, table, part, arrived, whole,
     wide, query, gq, gk, gv, go, weight, sampled, flipped, keys, values, attended, mine,
     ssend, srecv, tsend, trecv, lsend, lrecv, esend, erecv, bsend, brecv, zsend, zrecv,
-    asend, arecv, wsend, wrecv, dsend, drecv, osend, orecv,
+    asend, arecv, wsend, wrecv, dsend, drecv, osend, orecv, load_sem, own_sem, out_sem,
 ):
     head, band, dp = (lax.axis_index(name) for name in ("head", "band", "dp"))
     bands, heads = range(1, n_band), range(1, n_head)
@@ -118,6 +115,15 @@
     margin = KER // 2
     per_head = rows // n_head
     side_pad = 8
+    inputs = [(tok_in, tok), (gain_in, gain), (cr_in, cr), (cc_in, cc), (fr_in, fr), (taps_in, taps)]
+    loads = [pltpu.make_async_copy(src, dst, load_sem.at[k]) for k, (src, dst) in enumerate(inputs)]
+    owns = [
+        pltpu.make_async_copy(src.at[side], dst.at[side, head], own_sem.at[2 * k + side])
+        for k, (src, dst) in enumerate([(wq, gq), (wk, gk), (wv, gv), (wo, go)])
+        for side in range(2)
+    ]
+    for c in loads + owns:
+        c.start()
     greet(places)
 
     sems = (wsend, wrecv, dsend, drecv)
@@ -127,8 +133,8 @@
     copies = gather_start(early, head, dp, n_head, sems)
     after = {"band": shift(band, 1, n_band)}
     before = {"band": shift(band, n_band - 1, n_band)}
-    up = remote(tok.at[pl.ds(rows - margin, margin)], halo.at[0], lsend.at[0], lrecv.at[0], after)
-    down = remote(tok.at[pl.ds(0, margin)], halo.at[1], lsend.at[1], lrecv.at[1], before)
+    up = remote(tok_in.at[pl.ds(rows - margin, margin)], halo.at[0], lsend.at[0], lrecv.at[0], after)
+    down = remote(tok_in.at[pl.ds(0, margin)], halo.at[1], lsend.at[1], lrecv.at[1], before)
 
     @pl.when(band < n_band - 1)
     def _():
@@ -138,6 +144,8 @@
     def _():
         down.start()
 
+    for c in loads:
+        c.wait()
     for r in range(rows):
         mean, spread = stats_row(tok[r])
         stat[0:1, r * columns : (r + 1) * columns] = mean
@@ -153,7 +161,7 @@
     for off in heads:
         to = shift(head, off, n_head)
         c = remote(
-            tok.at[pl.ds(to * per_head, per_head)], xs.at[head], tsend.at[off - 1],
+            tok_in.at[pl.ds(to * per_head, per_head)], xs.at[head], tsend.at[off - 1],
             trecv.at[off - 1], {"head": to},
         )
         c.start()
@@ -180,7 +188,7 @@
     comb[...] = jnp.zeros_like(comb)
     side_comb[...] = jnp.zeros_like(side_comb)
 
-    for c in told:
+    for c in owns + told:
         c.wait()
     mean = stats[0, 0:1]
     for i in range(1, n_head):
@@ -293,6 +301,12 @@
     copies.update(gather_start(last, head, dp, n_head, sems))
     halves = gather_relay(early + later, copies, head, dp, n_head, sems)
     convolve(rows // 2, rows)
+    base_copy = pltpu.make_async_copy(base, base_out, out_sem.at[0])
+    base_copy.start()
+
+    @pl.loop(0, n_head * (channels // size))
+    def _(h):
+        values[h, :, channels:] = jnp.ones((points, channels), BF)
 
     for c in moved:
         c.wait()
@@ -340,7 +354,6 @@
             keys[i * group + j] = jnp.where(keep, key, 0.0).astype(BF)
             keep = (value_spot >= low_end) & (value_spot < high_end)
             values[i * group + j, :, 0:channels] = jnp.where(keep, value, 0.0).astype(BF)
-            values[i * group + j, :, channels:] = jnp.ones((points, channels), BF)
 
     halves = gather_relay(last, copies, head, dp, n_head, sems)
     gather_finish(copies, halves)
@@ -387,10 +400,13 @@
         for off in heads:
             back(step, off).start()
 
-    landed[head] = mine[head]
+    own_copy = pltpu.make_async_copy(mine.at[head], landed.at[head], out_sem.at[1])
+    own_copy.start()
+    base_copy.wait()
     for off in heads:
         for step in range(steps):
             back(step, off).wait()
+    own_copy.wait()
 
 
 def run_block(tokens, gain, cr, cc, fr, taps, wq, wk, wv, wo, n_head, n_band):
@@ -407,7 +423,10 @@
     factor = math.log2(math.e) / math.sqrt(size)
     V = pltpu.VMEM
     sem = pltpu.SemaphoreType.DMA
-    scratch = [
+    inputs = (tokens, gain, cr, cc, fr, taps)
+    scratch = [V(x.shape, x.dtype) for x in inputs]
+    scratch += [
+        V(tokens.shape, F32),
         V((n_head, per_head, columns, channels), BF),
         V((2, rows * columns), F32),
         V((n_head, 2, rows * columns), F32),
@@ -440,14 +459,15 @@
         (n_band, n_head - 1), (4, n_head - 1), (4, n_head - 1), (count // block, n_head - 1),
     ):
         scratch += [sem(shape)] * 2
+    scratch += [sem((len(inputs),)), sem((2 * len(weights),)), sem((2,))]
     return pl.pallas_call(
         functools.partial(block_kernel, size, factor, n_head, n_band),
         out_shape=[
             jax.ShapeDtypeStruct(tokens.shape, F32),
             jax.ShapeDtypeStruct((n_head, count, channels), BF),
         ],
-        in_specs=[VM] * 10,
-        out_specs=[VM] * 2,
+        in_specs=[pl.BlockSpec(memory_space=pltpu.HBM)] * 10,
+        out_specs=[pl.BlockSpec(memory_space=pltpu.HBM)] * 2,
         scratch_shapes=scratch,
         compiler_params=params(collective_id=0, has_side_effects=True),
         name="block",

time: 82.1 us -> 76.1 us (0.927)
  local copies, waits for them, and re-layouts: 8.31 us -> 0 us
  other arithmetic: 1.18 us -> 3.03 us
    unnamed x20 -> x0, local copies, waits for them, and re-layouts: 8.31 us -> none
    convert_element_type x1, other arithmetic: 1.18 us -> 3.03 us  [shards(): return (base + projected.reshape(tokens.shape).astype(F32)).astype(BF)]
where the time goes in v4:
time: 76.1 us; the launch traced here: 75.9 us
  Pallas kernels  72.9 us (96%)
  other arithmetic  3.03 us (4%)
    pallas_call x1, Pallas kernels, run_block(): pl.pallas_call(functools.partial(block_kernel, size, factor, n_head, n_ba...  72.9 us
    convert_element_type x1, other arithmetic, shards(): return (base + projected.reshape(tokens.shape).astype(F32)).astype(BF)  3.03 us

profile of v4, /device:TPU:0, one launch (start us, length us, event | category | flops | bytes accessed | tf_op | source)
XLA Modules:
  0.0 75.9 jit_solution(15442221440372942690)
XLA Ops:
  0.0 72.9 %block.1 = (f32[4,1024,128]{2,1,0:T(8,128)}, bf16[4,1024,128]{2,1,0:T(8,128)(2,1)}) custom-call(bf16[4,1024,128]{2,1,0:T(8,128)(2,1)} %tok_in.1, f32[4,1,128]{2,1,0:T(1,128)} %bitcast.13, s32[1,1024]{1,0:T(1,128)} %bitcast.11, s32[1,1024]{1,0:T(1,128)} %bitcast.12, f32[2,1024]{1,0:T(2,128)} %fr_in.1, f32[25,128]{1,0:T(8,128)} %taps_in.1, ...), custom_call_target="tpu_custom_call" | custom-call | tf_op jit(solution)/shard_map/block/pallas_call | solution.py:463
  72.9 3.0 %add_convert_fusion = bf16[4,1024,128]{2,1,0:T(8,128)(2,1)} fusion(f32[4,1024,128]{2,1,0:T(8,128)} %get-tuple-element.7, bf16[4,1024,128]{2,1,0:T(8,128)(2,1)} %get-tuple-element.8), kind=kLoop, calls=%fused_computation | loop fusion | flops 1572864 | bytes 4194304 | tf_op jit(solution)/shard_map/convert_element_type | solution.py:486

commit v5 on v4

--- a/solution.py
+++ b/solution.py
@@ -253,7 +253,7 @@
                         total = total + taps[a * KER + b : a * KER + b + 1, :] * padded[
                             r + a, pl.ds(begin + (side_pad - margin + b), tile), :
                         ]
-                base[r, at, :] = total
+                base[r, at, :] = total.astype(BF)
 
     rim_up.wait()
     rim_down.wait()
@@ -426,7 +426,7 @@
     inputs = (tokens, gain, cr, cc, fr, taps)
     scratch = [V(x.shape, x.dtype) for x in inputs]
     scratch += [
-        V(tokens.shape, F32),
+        V(tokens.shape, BF),
         V((n_head, per_head, columns, channels), BF),
         V((2, rows * columns), F32),
         V((n_head, 2, rows * columns), F32),
@@ -463,7 +463,7 @@
     return pl.pallas_call(
         functools.partial(block_kernel, size, factor, n_head, n_band),
         out_shape=[
-            jax.ShapeDtypeStruct(tokens.shape, F32),
+            jax.ShapeDtypeStruct(tokens.shape, BF),
             jax.ShapeDtypeStruct((n_head, count, channels), BF),
         ],
         in_specs=[pl.BlockSpec(memory_space=pltpu.HBM)] * 10,
@@ -483,7 +483,7 @@
         tokens, norm_gain.reshape(n_head, 1, channels), corner_row[None], corner_col[None], fraction,
         conv_kernel, w_query, w_key, w_value, w_out, n_head, n_band,
     )
-    return (base + projected.reshape(tokens.shape).astype(F32)).astype(BF)
+    return (base.astype(F32) + projected.reshape(tokens.shape).astype(F32)).astype(BF)
 
 
 def solution(mesh):

time: 76.1 us -> 75.8 us (level)
  no operation moved by 1% of the time
where the time goes in v5:
time: 75.8 us; the launch traced here: 75.7 us
  Pallas kernels  72.9 us (96%)
  other arithmetic  2.78 us (4%)
    pallas_call x1, Pallas kernels, run_block(): pl.pallas_call(functools.partial(block_kernel, size, factor, n_head, n_ba...  72.9 us
    convert_element_type x1, other arithmetic, shards(): (base.astype(F32) + projected.reshape(tokens.shape).astype(F32)).astype(BF)  2.78 us

profile of v5, /device:TPU:0, one launch (start us, length us, event | category | flops | bytes accessed | tf_op | source)
XLA Modules:
  0.0 75.7 jit_solution(4872750151521667820)
XLA Ops:
  0.0 72.9 %block.1 = (bf16[4,1024,128]{2,1,0:T(8,128)(2,1)}, bf16[4,1024,128]{2,1,0:T(8,128)(2,1)}) custom-call(bf16[4,1024,128]{2,1,0:T(8,128)(2,1)} %tok_in.1, f32[4,1,128]{2,1,0:T(1,128)} %bitcast.13, s32[1,1024]{1,0:T(1,128)} %bitcast.11, s32[1,1024]{1,0:T(1,128)} %bitcast.12, f32[2,1024]{1,0:T(2,128)} %fr_in.1, f32[25,128]{1,0:T(8,128)} %taps_in.1, ...), custom_call_target="tpu_custom_call" | custom-call | tf_op jit(solution)/shard_map/block/pallas_call | solution.py:463
  72.9 2.8 %add_convert_fusion = bf16[4,1024,128]{2,1,0:T(8,128)(2,1)} fusion(bf16[4,1024,128]{2,1,0:T(8,128)(2,1)} %get-tuple-element.8, bf16[4,1024,128]{2,1,0:T(8,128)(2,1)} %get-tuple-element.7), kind=kLoop, calls=%fused_computation | loop fusion | flops 2097152 | bytes 3145728 | tf_op jit(solution)/shard_map/convert_element_type | solution.py:486
